TPU v7x, 32 devices: a whole 2x2x4 slice. The times are simulated.
32 devices in a mesh: dp: 4 (over z), ctx: 4 (over x, core), tensor: 2 (over y).
Axes of the slice: x: 2, y: 2, z: 4, core: 2. Of those that a mesh axis runs over, the one named last changes fastest.
Arguments:
- layer_input: bfloat16 [4, 1024, 2048], P('dp', 'ctx'), may hold values from -6 to 6
- output_grad: bfloat16 [4, 1024, 2048], P('dp', 'ctx'), may hold values from -6 to 6
- prefix: int32 [4], P('dp'), may hold values from 204 to 1024
- attn_gain: float32 [2048], replicated, may hold values from 0.1 to 1.9
- w_query: bfloat16 [2048, 2048], P(None, 'tensor'), may hold values from -0.125 to 0.125
- w_key: bfloat16 [2048, 512], P(None, 'tensor'), may hold values from -0.125 to 0.125
- w_value: bfloat16 [2048, 512], P(None, 'tensor'), may hold values from -0.125 to 0.125
- w_out: bfloat16 [2048, 2048], P('tensor'), may hold values from -1 to 1
- mlp_gain: float32 [2048], replicated, may hold values from 0.1 to 1.9
- w_gate: bfloat16 [2048, 8192], P(None, 'tensor'), may hold values from -0.125 to 0.125
- w_up: bfloat16 [2048, 8192], P(None, 'tensor'), may hold values from -0.125 to 0.125
- w_down: bfloat16 [8192, 2048], P('tensor'), may hold values from -0.0625 to 0.0625
Outputs:
- layer_output: bfloat16 [4, 1024, 2048], P('dp', 'ctx')
- input_grad: float32 [4, 1024, 2048], P('dp', 'ctx')
- d_attn_gain: float32 [2048], P(('dp', 'ctx'))
- d_query: float32 [2048, 2048], P(('dp', 'ctx'), 'tensor')
- d_key: float32 [2048, 512], P(('dp', 'ctx'), 'tensor')
- d_value: float32 [2048, 512], P(('dp', 'ctx'), 'tensor')
- d_out_proj: float32 [2048, 2048], P('tensor', ('dp', 'ctx'))
- d_mlp_gain: float32 [2048], P(('dp', 'ctx'))
- d_gate: float32 [2048, 8192], P(('dp', 'ctx'), 'tensor')
- d_up: float32 [2048, 8192], P(('dp', 'ctx'), 'tensor')
- d_down: float32 [8192, 2048], P('tensor', ('dp', 'ctx'))
All inputs are finite; a program needn't handle non-finite values.
Results may differ from a plain program's by a relative error of at most 0.024.
Values may be sent and summed in bfloat16 or wider, within the bound.
A program may use at most 256 MiB of HBM per device.

v0:
```python
import jax
import jax.numpy as jnp
from jax import lax
from jax.sharding import PartitionSpec as P

HD = 64


EPS = 1e-05
ROPE_BASE = 500000.0
NEG = -1e30


def dot_plain(left, right):
    return jnp.dot(left, right, preferred_element_type=jnp.float32)


def dot_right(left, right):
    return lax.dot_general(
        left, right, (((1,), (1,)), ((), ())), preferred_element_type=jnp.float32
    )


def dot_left(left, right):
    return lax.dot_general(
        left, right, (((0,), (0,)), ((), ())), preferred_element_type=jnp.float32
    )


def normed(v, gain):
    return v * lax.rsqrt(jnp.mean(v * v, axis=-1, keepdims=True) + EPS) * gain


def norm_back(v, gain, grad):
    factor = lax.rsqrt(jnp.mean(v * v, axis=-1, keepdims=True) + EPS)
    unit = v * factor
    d_unit = grad * gain
    d_gain = jnp.sum(grad * unit, axis=0)
    d_v = factor * (d_unit - unit * jnp.mean(d_unit * unit, axis=-1, keepdims=True))
    return (d_v, d_gain)


def rotate(t, cosine, sine):
    half = t.shape[-1] // 2
    first, second = (t[..., :half], t[..., half:])
    return jnp.concatenate(
        [first * cosine - second * sine, second * cosine + first * sine], axis=-1
    )


def rotate_back(t, cosine, sine):
    half = t.shape[-1] // 2
    first, second = (t[..., :half], t[..., half:])
    return jnp.concatenate(
        [first * cosine + second * sine, second * cosine - first * sine], axis=-1
    )


def score_block(query5, key_all, allowed):
    scores = jnp.einsum(
        "scngd,slnd->sngcl", query5, key_all, preferred_element_type=jnp.float32
    ) * HD ** (-0.5)
    return jnp.where(allowed[:, None, None], scores, NEG)


def forward(
    rows,
    prefix,
    attn_gain,
    w_query,
    w_key,
    w_value,
    w_out,
    mlp_gain,
    w_gate,
    w_up,
    w_down,
    seqs,
    span,
):
    q_heads = w_query.shape[1] // HD
    kv_heads = w_key.shape[1] // HD
    group = q_heads // kv_heads
    first = lax.axis_index("ctx") * span
    position = (first + jnp.arange(span)).astype(jnp.float32)
    frequency = ROPE_BASE ** (-jnp.arange(HD // 2).astype(jnp.float32) * 2.0 / HD)
    angle = position[:, None] * frequency[None, :]
    cosine = jnp.cos(angle)[None, :, None, :]
    sine = jnp.sin(angle)[None, :, None, :]
    normed1 = normed(rows, attn_gain).astype(jnp.bfloat16)
    query = rotate(
        dot_plain(normed1, w_query).reshape(seqs, span, q_heads, HD), cosine, sine
    ).astype(jnp.bfloat16)
    keyed = rotate(
        dot_plain(normed1, w_key).reshape(seqs, span, kv_heads, HD), cosine, sine
    ).astype(jnp.bfloat16)
    valued = dot_plain(normed1, w_value).astype(jnp.bfloat16).reshape(seqs, span, kv_heads * HD)
    key_all, value_all = (
        lax.all_gather(keyed.reshape(seqs, span, kv_heads * HD), "ctx", axis=1, tiled=True),
        lax.all_gather(valued, "ctx", axis=1, tiled=True),
    )
    length = key_all.shape[1]
    key_all = key_all.reshape(seqs, length, kv_heads, HD)
    value_all = value_all.reshape(seqs, length, kv_heads, HD)
    query5 = query.reshape(seqs, span, kv_heads, group, HD)
    query_pos = first + jnp.arange(span)
    key_pos = jnp.arange(length)
    allowed = (key_pos[None, None, :] <= query_pos[None, :, None]) | (
        key_pos[None, None, :] < prefix[:, None, None]
    )
    scores = score_block(query5, key_all, allowed)
    top = jnp.max(scores, axis=-1, keepdims=True)
    exponent = jnp.exp(scores - top)
    total = jnp.sum(exponent, axis=-1, keepdims=True)
    log_total = top + jnp.log(total)
    probs_low = (exponent / total).astype(jnp.bfloat16)
    attended = jnp.einsum(
        "sngcl,slnd->scngd", probs_low, value_all, preferred_element_type=jnp.float32
    )
    attended = attended.astype(jnp.bfloat16).reshape(seqs * span, q_heads * HD)
    resid = rows + lax.psum(dot_plain(attended, w_out), "tensor")
    normed2 = normed(resid, mlp_gain).astype(jnp.bfloat16)
    gate = dot_plain(normed2, w_gate)
    up = dot_plain(normed2, w_up)
    act = (jax.nn.silu(gate) * up).astype(jnp.bfloat16)
    result = resid + lax.psum(dot_plain(act, w_down).astype(jnp.bfloat16), "tensor").astype(
        jnp.float32
    )
    kept = (
        normed1,
        query5,
        key_all,
        value_all,
        log_total,
        allowed,
        attended,
        resid,
        normed2,
        gate,
        up,
        act,
        cosine,
        sine,
    )
    return (result, kept)


def local(
    layer_input,
    output_grad,
    prefix,
    attn_gain,
    w_query,
    w_key,
    w_value,
    w_out,
    mlp_gain,
    w_gate,
    w_up,
    w_down,
):
    seqs, span, width = layer_input.shape
    rows = layer_input.astype(jnp.float32).reshape(seqs * span, width)
    result, kept = forward(
        rows,
        prefix,
        attn_gain,
        w_query,
        w_key,
        w_value,
        w_out,
        mlp_gain,
        w_gate,
        w_up,
        w_down,
        seqs,
        span,
    )
    output = result.astype(jnp.bfloat16)
    output = output.reshape(seqs, span, width)
    unused, kept = forward(
        rows,
        prefix,
        attn_gain,
        w_query,
        w_key,
        w_value,
        w_out,
        mlp_gain,
        w_gate,
        w_up,
        w_down,
        seqs,
        span,
    )
    (
        normed1,
        query5,
        key_all,
        value_all,
        log_total,
        allowed,
        attended,
        resid,
        normed2,
        gate,
        up,
        act,
        cosine,
        sine,
    ) = kept
    kv_heads = key_all.shape[2]
    q_heads = w_query.shape[1] // HD
    length = key_all.shape[1]
    grad_low = output_grad.reshape(seqs * span, width)
    grad_rows = grad_low.astype(jnp.float32)
    g_down = dot_left(act, grad_low)
    d_act = dot_right(grad_low, w_down)
    sigmoid_gate = jax.nn.sigmoid(gate)
    d_gate_pre = (d_act * up * sigmoid_gate * (1.0 + gate * (1.0 - sigmoid_gate))).astype(
        jnp.bfloat16
    )
    d_up_pre = (d_act * gate * sigmoid_gate).astype(jnp.bfloat16)
    g_gate = dot_left(normed2, d_gate_pre)
    g_up = dot_left(normed2, d_up_pre)
    back_terms = dot_right(d_gate_pre, w_gate) + dot_right(d_up_pre, w_up)
    d_normed2 = lax.psum(back_terms.astype(jnp.bfloat16), "tensor").astype(jnp.float32)
    d_resid_norm, g_mlp_gain = norm_back(resid, mlp_gain, d_normed2)
    d_resid = grad_rows + d_resid_norm
    d_resid_low = d_resid.astype(jnp.bfloat16)
    g_out = dot_left(attended, d_resid_low)
    d_attended = dot_right(d_resid_low, w_out).astype(jnp.bfloat16).reshape(query5.shape)
    scores = score_block(query5, key_all, allowed)
    probs = jnp.exp(scores - log_total)
    probs_low = probs.astype(jnp.bfloat16)
    d_probs = jnp.einsum(
        "scngd,slnd->sngcl", d_attended, value_all, preferred_element_type=jnp.float32
    )
    delta = jnp.sum(probs * d_probs, axis=-1, keepdims=True)
    d_scores = (probs * (d_probs - delta)).astype(jnp.bfloat16)
    scale = HD ** (-0.5)
    d_query = (
        jnp.einsum("sngcl,slnd->scngd", d_scores, key_all, preferred_element_type=jnp.float32)
        * scale
    )
    d_key_all = (
        jnp.einsum("sngcl,scngd->slnd", d_scores, query5, preferred_element_type=jnp.float32)
        * scale
    )
    d_value_all = jnp.einsum(
        "sngcl,scngd->slnd", probs_low, d_attended, preferred_element_type=jnp.float32
    )
    d_key, d_val = (
        lax.psum_scatter(
            d_key_all.reshape(seqs, length, kv_heads * HD).astype(jnp.bfloat16),
            "ctx",
            scatter_dimension=1,
            tiled=True,
        ).astype(jnp.float32),
        lax.psum_scatter(
            d_value_all.reshape(seqs, length, kv_heads * HD).astype(jnp.bfloat16),
            "ctx",
            scatter_dimension=1,
            tiled=True,
        ).astype(jnp.float32),
    )
    d_qp = (
        rotate_back(d_query.reshape(seqs, span, q_heads, HD), cosine, sine)
        .astype(jnp.bfloat16)
        .reshape(seqs * span, q_heads * HD)
    )
    d_kp = (
        rotate_back(d_key.reshape(seqs, span, kv_heads, HD), cosine, sine)
        .astype(jnp.bfloat16)
        .reshape(seqs * span, kv_heads * HD)
    )
    d_vp = d_val.astype(jnp.bfloat16).reshape(seqs * span, kv_heads * HD)
    g_query = dot_left(normed1, d_qp)
    g_key = dot_left(normed1, d_kp)
    g_value = dot_left(normed1, d_vp)
    front_terms = dot_right(d_qp, w_query) + dot_right(d_kp, w_key) + dot_right(d_vp, w_value)
    d_normed1 = lax.psum(front_terms.astype(jnp.bfloat16), "tensor").astype(jnp.float32)
    d_rows_norm, g_attn_gain = norm_back(rows, attn_gain, d_normed1)
    d_input = d_resid + d_rows_norm
    d_input = d_input.reshape(seqs, span, width)
    s_attn_gain, s_query, s_key, s_value, s_out, s_mlp_gain, s_gate, s_up, s_down = (
        lax.psum_scatter(
            g_attn_gain.astype(jnp.bfloat16), ("dp", "ctx"), scatter_dimension=0, tiled=True
        ).astype(jnp.float32),
        lax.psum_scatter(
            g_query.astype(jnp.bfloat16), ("dp", "ctx"), scatter_dimension=0, tiled=True
        ).astype(jnp.float32),
        lax.psum_scatter(
            g_key.astype(jnp.bfloat16), ("dp", "ctx"), scatter_dimension=0, tiled=True
        ).astype(jnp.float32),
        lax.psum_scatter(
            g_value.astype(jnp.bfloat16), ("dp", "ctx"), scatter_dimension=0, tiled=True
        ).astype(jnp.float32),
        lax.psum_scatter(
            g_out.astype(jnp.bfloat16), ("dp", "ctx"), scatter_dimension=1, tiled=True
        ).astype(jnp.float32),
        lax.psum_scatter(
            g_mlp_gain.astype(jnp.bfloat16), ("dp", "ctx"), scatter_dimension=0, tiled=True
        ).astype(jnp.float32),
        lax.psum_scatter(
            g_gate.astype(jnp.bfloat16), ("dp", "ctx"), scatter_dimension=0, tiled=True
        ).astype(jnp.float32),
        lax.psum_scatter(
            g_up.astype(jnp.bfloat16), ("dp", "ctx"), scatter_dimension=0, tiled=True
        ).astype(jnp.float32),
        lax.psum_scatter(
            g_down.astype(jnp.bfloat16), ("dp", "ctx"), scatter_dimension=1, tiled=True
        ).astype(jnp.float32),
    )
    return (
        output,
        d_input,
        s_attn_gain,
        s_query,
        s_key,
        s_value,
        s_out,
        s_mlp_gain,
        s_gate,
        s_up,
        s_down,
    )


def solution(mesh):
    return jax.shard_map(
        local,
        mesh=mesh,
        in_specs=(
            P("dp", "ctx", None),
            P("dp", "ctx", None),
            P("dp"),
            P(),
            P(None, "tensor"),
            P(None, "tensor"),
            P(None, "tensor"),
            P("tensor", None),
            P(),
            P(None, "tensor"),
            P(None, "tensor"),
            P("tensor", None),
        ),
        out_specs=(
            P("dp", "ctx", None),
            P("dp", "ctx", None),
            P(("dp", "ctx")),
            P(("dp", "ctx"), "tensor"),
            P(("dp", "ctx"), "tensor"),
            P(("dp", "ctx"), "tensor"),
            P("tensor", ("dp", "ctx")),
            P(("dp", "ctx")),
            P(("dp", "ctx"), "tensor"),
            P(("dp", "ctx"), "tensor"),
            P("tensor", ("dp", "ctx")),
        ),
        check_vma=False,
    )
```

profile of v0, /device:TPU:25, one launch (start us, length us, event | category | flops | bytes accessed | tf_op | source)
XLA Modules:
  0.0 1190.9 jit_solution(372620300648017163)
XLA Ops:
  11.3 7.7 all_gather.9
  19.0 6.7 copy.43
  30.6 7.3 all-gather
  38.4 7.2 fusion.73
  45.5 8.0 fusion.3
  53.6 7.5 fusion.44
  64.1 62.7 %all-reduce.8.cloned.1.call-done = f32[256,2048]{1,0:T(8,128)} async-done(((f32[256,2048]{1,0:T(8,128)}), f32[256,2048]{1,0:T(8,128)}) %all-reduce.8.cloned.1.call-update) | async-done | bytes 2097168 | tf_op jit(solution)/shard_map/psum | solution.py:121
  129.4 10.8 fusion.75
  141.6 6.1 fusion.76
  147.7 13.3 %multiply_convert_fusion = (bf16[256,4096]{1,0:T(8,128)(2,1)}, bf16[256,4096]{1,0:T(8,128)(2,1)}, bf16[256,4096]{1,0:T(8,128)(2,1)}) fusion(f32[256,4096]{1,0:T(8,128)} %fusion.75, f32[256,4096]{1,0:T(8,128)} %fusion.76, bf16[4096,2048]{1,0:T(8,128)(2,1)} %param.23, bf16[1,256,2048]{2,1,0:T(8,128)(2,1)S(1)} %copy-done.8), kind=kOutput, calls=%fused_computation.20 | convolution fusion | flops 4311744512 | bytes 32505856 | tf_op jit(solution)/shard_map/dot_general | solution.py:19
  161.1 12.2 %fusion.77 = f32[256,2048]{1,0:T(8,128)} fusion(bf16[256,4096]{1,0:T(8,128)(2,1)} %get-tuple-element.22, bf16[2048,4096]{1,0:T(8,128)(2,1)} %param.21), kind=kOutput, calls=%fused_computation.124 | convolution fusion | flops 4294967296 | bytes 20971520 | tf_op jit(solution)/shard_map/dot_general | solution.py:19
  173.3 12.5 %fusion.18 = bf16[256,2048]{1,0:T(8,128)(2,1)} fusion(f32[256,2048]{1,0:T(8,128)} %fusion.77, bf16[256,4096]{1,0:T(8,128)(2,1)} %get-tuple-element.21, bf16[2048,4096]{1,0:T(8,128)(2,1)} %param.22), kind=kOutput, calls=%fused_computation.41 | convolution fusion | flops 4296015872 | bytes 22020096 | tf_op jit(solution)/shard_map/dot_general | solution.py:19
  186.3 39.7 %all-reduce.10.cloned.1.call-done = bf16[256,2048]{1,0:T(8,128)(2,1)} async-done(((bf16[256,2048]{1,0:T(8,128)(2,1)}), bf16[256,2048]{1,0:T(8,128)(2,1)}) %all-reduce.10.cloned.1.call-update) | async-done | bytes 1048592 | tf_op jit(solution)/shard_map/psum | solution.py:227
  235.3 9.5 fusion.40
  244.8 10.7 fusion
  255.6 12.0 %fusion.8 = bf16[4,4,256,1024]{2,3,1,0:T(8,128)(2,1)S(1)} fusion(f32[4,1024,256,4]{2,1,3,0:T(8,128)} %get-tuple-element.37, f32[1,4,4,256,1024]{3,4,2,1,0:T(8,128)} %get-tuple-element.35, f32[4,4,256]{2,1,0:T(4,128)S(1)} %get-tuple-element.36, f32[4,4,256]{2,1,0:T(4,128)S(1)} %bitcast.223), kind=kLoop, calls=%fused_computation.16 | loop fusion | flops 16777216 | bytes 41975808 | tf_op jit(solution)/shard_map/reshape.27
  271.2 6.1 reduce-scatter.16.cloned.1.call-done
  280.5 11.9 %convolution_convert_fusion.5 = bf16[256,2048]{1,0:T(8,128)(2,1)} fusion(bf16[256,4096]{1,0:T(8,128)(2,1)} %get-tuple-element.23, bf16[4096,2048]{1,0:T(8,128)(2,1)} %param.23), kind=kOutput, calls=%fused_computation.42 | convolution fusion | flops 4295491584 | bytes 19922944 | tf_op jit(solution)/shard_map/dot_general | solution.py:15
  292.4 9.5 reduce-scatter.14.cloned.1.call-done
  320.2 6.5 copy.57
  331.8 12.3 %convolution_convert_fusion = bf16[4096,2048]{1,0:T(8,128)(2,1)} fusion(bf16[256,4096]{1,0:T(8,128)(2,1)} %get-tuple-element.23, bf16[1,256,2048]{2,1,0:T(8,128)(2,1)} %param.13), kind=kOutput, calls=%fused_computation.9 | convolution fusion | flops 4303355904 | bytes 19922944 | tf_op jit(solution)/shard_map/dot_general | solution.py:25
  344.1 20.9 %copy.59 = bf16[4096,2048]{0,1:T(8,128)(2,1)} copy(bf16[4096,2048]{1,0:T(8,128)(2,1)} %convolution_convert_fusion) | data formatting | bytes 33554432
  365.1 12.3 %convolution_convert_fusion.2 = bf16[2048,4096]{1,0:T(8,128)(2,1)} fusion(bf16[256,2048]{1,0:T(8,128)(2,1)} %copy-done.4, bf16[256,4096]{1,0:T(8,128)(2,1)} %get-tuple-element.22), kind=kOutput, calls=%fused_computation.11 | convolution fusion | flops 4303355904 | bytes 19922944 | tf_op jit(solution)/shard_map/dot_general | solution.py:25
  377.7 12.3 %convolution_convert_fusion.1 = bf16[2048,4096]{1,0:T(8,128)(2,1)} fusion(bf16[256,2048]{1,0:T(8,128)(2,1)} %copy-done.4, bf16[256,4096]{1,0:T(8,128)(2,1)} %get-tuple-element.21), kind=kOutput, calls=%fused_computation.10 | convolution fusion | flops 4303355904 | bytes 19922944 | tf_op jit(solution)/shard_map/dot_general | solution.py:25
  393.4 27.0 %reduce-scatter.20.cloned.1.call-done = bf16[128,256]{1,0:T(8,128)(2,1)} async-done(((bf16[2048,256]{1,0:T(8,128)(2,1)}), bf16[128,256]{1,0:T(8,128)(2,1)}) %reduce-scatter.20.cloned.1.call-update) | async-done | bytes 65552 | tf_op jit(solution)/shard_map/reduce_scatter | solution.py:293
  421.9 66.3 %all-reduce.12.cloned.1.call-done = (bf16[256,2048]{1,0:T(8,128)(2,1)}, bf16[256,2048]{1,0:T(8,128)(2,1)}) async-done(((bf16[256,2048]{1,0:T(8,128)(2,1)}, bf16[256,2048]{1,0:T(8,128)(2,1)}), (bf16[256,2048]{1,0:T(8,128)(2,1)}, bf16[256,2048]{1,0:T(8,128)(2,1)})) %all-reduce.12.cloned.1.call-update) | async-done | bytes 2097168 | tf_op jit(solution)/shard_map/psum | solution.py:126
  490.5 26.0 %all-reduce.2 = (bf16[2048]{0:T(1024)(128)(2,1)S(1)}, bf16[2048]{0:T(1024)(128)(2,1)S(1)}) all-reduce(bf16[2048]{0:T(1024)(128)(2,1)S(1)} %get-tuple-element.13, bf16[2048]{0:T(1024)(128)(2,1)S(1)} %get-tuple-element.11), channel_id=5, replica_groups=mesh['dp'=4,'ctx'=4,'tensor'=2] {'dp','ctx'}, use_global_device_ids=true, to_apply=%region_14.15.clone | all-reduce | flops 4096 | bytes 16384
  522.3 40.1 %reduce-scatter.28.cloned.1.call-done = bf16[128,1024]{1,0:T(8,128)(2,1)} async-done(((bf16[2048,1024]{1,0:T(8,128)(2,1)}), bf16[128,1024]{1,0:T(8,128)(2,1)}) %reduce-scatter.28.cloned.1.call-update) | async-done | bytes 262160
  564.3 73.8 %reduce-scatter.18.cloned.1.call-done = bf16[128,1024]{1,0:T(8,128)(2,1)} async-done(((bf16[2048,1024]{1,0:T(8,128)(2,1)}), bf16[128,1024]{1,0:T(8,128)(2,1)}) %reduce-scatter.18.cloned.1.call-update) | async-done | bytes 262160 | tf_op jit(solution)/shard_map/reduce_scatter | solution.py:290
  639.9 179.9 %reduce-scatter.30.cloned.1.call-done = bf16[128,4096]{1,0:T(8,128)(2,1)} async-done(((bf16[2048,4096]{1,0:T(8,128)(2,1)}), bf16[128,4096]{1,0:T(8,128)(2,1)}) %reduce-scatter.30.cloned.1.call-update) | async-done | bytes 1048592
  822.9 177.5 %reduce-scatter.24.cloned.1.call-done = bf16[128,4096]{1,0:T(8,128)(2,1)} async-done(((bf16[2048,4096]{1,0:T(8,128)(2,1)}), bf16[128,4096]{1,0:T(8,128)(2,1)}) %reduce-scatter.24.cloned.1.call-update) | async-done | bytes 1048592 | tf_op jit(solution)/shard_map/reduce_scatter | solution.py:305
  1003.1 177.7 %reduce-scatter.26.cloned.1.call-done = bf16[128,4096]{1,0:T(8,128)(2,1)} async-done(((bf16[2048,4096]{1,0:T(8,128)(2,1)}), bf16[128,4096]{1,0:T(8,128)(2,1)}) %reduce-scatter.26.cloned.1.call-update) | async-done | bytes 1048592 | tf_op jit(solution)/shard_map/reduce_scatter | solution.py:308
  (136 shorter events, 80.2 us)
Async XLA Ops:
  7.2 22.9 %copy-start = (bf16[2048,256]{1,0:T(8,128)(2,1)S(1)}, bf16[2048,256]{1,0:T(8,128)(2,1)}, u32[]{:S(2)}) copy-start(bf16[2048,256]{1,0:T(8,128)(2,1)} %param.18) | copy-start | bytes 3145732
  7.2 3.5 copy-start.2
  7.2 3.5 copy-start.18
  7.2 119.6 %all-reduce.8.cloned.1.call-start = ((), (), s32[]{:S(2)}) async-start(), calls=%async_computation.9 | async-start | bytes 4194304 | tf_op jit(solution)/shard_map/psum | solution.py:121
  19.0 19.4 %copy-start.6 = (bf16[1,1024,256]{1,2,0:T(8,128)(2,1)}, bf16[1,1024,256]{1,2,0:T(8,128)(2,1)S(1)}, u32[]{:S(2)}) copy-start(bf16[1,1024,256]{1,2,0:T(8,128)(2,1)S(1)} %all_gather.9) | copy-start | bytes 1572868
  29.5 8.9 copy-start.12
  38.1 15.5 %copy-start.14 = (bf16[1024,256]{0,1:T(8,128)(2,1)}, bf16[1024,256]{0,1:T(8,128)(2,1)S(1)}, u32[]{:S(2)}) copy-start(bf16[1024,256]{0,1:T(8,128)(2,1)S(1)} %copy.41) | copy-start | bytes 1572868
  53.6 7.6 copy-start.21
  63.8 65.2 %copy-start.20 = (f32[2048]{0:T(1024)S(1)}, f32[2048]{0:T(1024)}, u32[]{:S(2)}) copy-start(f32[2048]{0:T(1024)} %param.20) | copy-start | bytes 24580
  63.8 162.2 %all-reduce.10.cloned.1.call-start = ((), (), s32[]{:S(2)}) async-start(), calls=%async_computation.10 | async-start | bytes 2097152 | tf_op jit(solution)/shard_map/psum | solution.py:227
  129.1 11.1 slice-start
  129.3 10.9 copy-start.4
  129.3 10.9 slice-start.1
  129.3 10.9 slice-start.2
  129.4 12.2 %slice-start.3 = ((s8[16777216]{0:T(1024)(128)(4,1)}), s8[4194304]{0:T(1024)(128)(4,1)S(1)}, s32[]{:S(2)}) async-start(s8[16777216]{0:T(1024)(128)(4,1)} %bitcast.228), calls=%async_computation.24 | async-start | bytes 8388608
  141.6 6.1 copy-start.8
  185.8 91.6 %reduce-scatter.16.cloned.1.call-start = ((), (), s32[]{:S(2)}) async-start(), calls=%async_computation.12 | async-start | bytes 655360 | tf_op jit(solution)/shard_map/reduce_scatter | solution.py:260
  228.2 2.9 copy-start.22
  235.3 9.5 copy-start.5
  235.3 9.5 copy-start.15
  255.5 46.4 %reduce-scatter.14.cloned.1.call-start = ((), (), s32[]{:S(2)}) async-start(), calls=%async_computation.11 | async-start | bytes 655360 | tf_op jit(solution)/shard_map/reduce_scatter | solution.py:254
  255.6 12.0 %copy-start.13 = (bf16[1,256,16,32]{1,3,2,0:T(8,128)(2,1)S(1)}, bf16[1,256,16,32]{1,3,2,0:T(8,128)(2,1)}, u32[]{:S(2)}) copy-start(bf16[1,256,16,32]{1,3,2,0:T(8,128)(2,1)} %copy-done.12) | copy-start | bytes 786436
  267.6 3.6 copy-start.1
  271.2 120.7 %reduce-scatter.22.cloned.1.call-start = ((), (), s32[]{:S(2)}) async-start(), calls=%async_computation.15 | async-start | bytes 1114112 | tf_op jit(solution)/shard_map/reduce_scatter | solution.py:296
  280.2 140.2 %reduce-scatter.20.cloned.1.call-start = ((), (), s32[]{:S(2)}) async-start(), calls=%async_computation.14 | async-start | bytes 1114112 | tf_op jit(solution)/shard_map/reduce_scatter | solution.py:293
  305.7 182.4 %all-reduce.12.cloned.1.call-start = ((), (), s32[]{:S(2)}) async-start(), calls=%async_computation.20 | async-start | bytes 4194304 | tf_op jit(solution)/shard_map/psum | solution.py:126
  305.8 5.5 copy-start.7
  315.1 247.2 %reduce-scatter.28.cloned.1.call-start = ((), (), s32[]{:S(2)}) async-start(), calls=%async_computation.18 | async-start | bytes 4456448
  326.7 311.4 %reduce-scatter.18.cloned.1.call-start = ((), (), s32[]{:S(2)}) async-start(), calls=%async_computation.13 | async-start | bytes 4456448 | tf_op jit(solution)/shard_map/reduce_scatter | solution.py:290
  331.5 488.3 %reduce-scatter.30.cloned.1.call-start = ((), (), s32[]{:S(2)}) async-start(), calls=%async_computation.19 | async-start | bytes 17825792
  365.0 635.4 %reduce-scatter.24.cloned.1.call-start = ((), (), s32[]{:S(2)}) async-start(), calls=%async_computation.16 | async-start | bytes 17825792 | tf_op jit(solution)/shard_map/reduce_scatter | solution.py:305
  377.4 803.4 %reduce-scatter.26.cloned.1.call-start = ((), (), s32[]{:S(2)}) async-start(), calls=%async_computation.17 | async-start | bytes 17825792 | tf_op jit(solution)/shard_map/reduce_scatter | solution.py:308
  (8 other events, 12.6 us)
Sparse Core Ops, SparseCore 0:
  63.9 62.8 all-reduce.7
  185.9 40.0 all-reduce.9
  255.7 21.6 reduce-scatter.15
  280.3 21.6 reduce-scatter.13
  305.4 54.8 reduce-scatter.21
  363.7 56.6 reduce-scatter.19
  423.3 64.8 all-reduce.11
  492.0 70.2 reduce-scatter.27
  566.2 71.8 reduce-scatter.17
  642.0 177.7 reduce-scatter.29
  823.9 176.4 reduce-scatter.23
  1004.4 176.4 reduce-scatter.25
where the time goes:
time: 1200 us; the launch traced here: 1190 us
  waiting for transfers between devices  861 us (72%)
  matrix products  175 us (15%)
  other arithmetic  49.5 us (4%)
  local copies, waits for them, and re-layouts  46.1 us (4%)
  blocking collectives  40.9 us (3%)
  between operations  16.5 us (1%)
    unnamed x14, waiting for transfers between devices  220 us
    reduce_scatter x1, waiting for transfers between devices, local(): lax.psum_scatter(g_up.astype(jnp.bfloat16), ('dp', 'ctx'), scatter_dimens...  178 us
    reduce_scatter x1, waiting for transfers between devices, local(): lax.psum_scatter(g_gate.astype(jnp.bfloat16), ('dp', 'ctx'), scatter_dime...  178 us
    reduce_scatter x1, waiting for transfers between devices, local(): lax.psum_scatter(g_query.astype(jnp.bfloat16), ('dp', 'ctx'), scatter_dim...  73.8 us
    psum x1, waiting for transfers between devices, forward(): lax.psum(dot_plain(act, w_down).astype(jnp.bfloat16), 'tensor')  66.3 us
    psum x1, waiting for transfers between devices, forward(): resid = rows + lax.psum(dot_plain(attended, w_out), 'tensor')  62.7 us
    dot_general x7, matrix products, dot_left(): lax.dot_general(left, right, (((0,), (0,)), ((), ())), preferred_element_...  52.3 us
    unnamed x63, local copies, waits for them, and re-layouts  43.8 us
  transfers between devices with their start and end apart: 12, of which 11 were waited for; matrix products, arithmetic and copies ran while one was open for 12% of the time, Pallas kernels for 0%

commit v1 on v0

v1 whole, which is shorter than its diff:
```python
import jax
import jax.numpy as jnp
from jax import lax
from jax.sharding import PartitionSpec as P

HD = 64


EPS = 1e-05
ROPE_BASE = 500000.0
NEG = -1e30
BF = jnp.bfloat16
F32 = jnp.float32


def dot_plain(left, right):
    return jnp.dot(left, right, preferred_element_type=F32)


def dot_right(left, right):
    return lax.dot_general(left, right, (((1,), (1,)), ((), ())), preferred_element_type=F32)


def dot_left(left, right):
    return lax.dot_general(left, right, (((0,), (0,)), ((), ())), preferred_element_type=F32)


def normed(v, gain):
    return v * lax.rsqrt(jnp.mean(v * v, axis=-1, keepdims=True) + EPS) * gain


def norm_back(v, gain, grad):
    factor = lax.rsqrt(jnp.mean(v * v, axis=-1, keepdims=True) + EPS)
    unit = v * factor
    d_unit = grad * gain
    d_gain = jnp.sum(grad * unit, axis=0)
    d_v = factor * (d_unit - unit * jnp.mean(d_unit * unit, axis=-1, keepdims=True))
    return (d_v, d_gain)


def rotate(t, cosine, sine):
    half = t.shape[-1] // 2
    first, second = (t[..., :half], t[..., half:])
    return jnp.concatenate(
        [first * cosine - second * sine, second * cosine + first * sine], axis=-1
    )


def rotate_back(t, cosine, sine):
    half = t.shape[-1] // 2
    first, second = (t[..., :half], t[..., half:])
    return jnp.concatenate(
        [first * cosine + second * sine, second * cosine - first * sine], axis=-1
    )


def score_block(query5, key_all, allowed):
    scores = jnp.einsum(
        "scngd,slnd->sngcl", query5, key_all, preferred_element_type=F32
    ) * HD ** (-0.5)
    return jnp.where(allowed[:, None, None], scores, NEG)


def build(ndp, nctx, nten):
    def pull(v, axis, n, s):
        return lax.ppermute(v, axis, [((i + s) % n, i) for i in range(n)])

    def flip(v, axis, n, bit):
        return lax.ppermute(v, axis, [(i, i ^ bit) for i in range(n)])

    def tensor_sum(v):
        low = v.astype(BF)
        if nten == 2:
            return low.astype(F32) + flip(low, "tensor", 2, 1).astype(F32)
        return lax.psum(low, "tensor").astype(F32)

    def gather_dp(v):
        rows = v.shape[0] // nten
        part = lax.dynamic_slice_in_dim(v, lax.axis_index("tensor") * rows, rows, 0)
        pieces = [v]
        for s in range(1, ndp):
            got = pull(part, "dp", ndp, s)
            pieces.append(got)
            for t in range(1, nten):
                pieces.append(pull(got, "tensor", nten, t))
        return jnp.concatenate(pieces, axis=0)

    def ctx_sum(full):
        r = full.shape[0] // (ndp * nctx)
        me = lax.axis_index("ctx")
        work = full.reshape(ndp, nctx, r, full.shape[1])
        bit = 1
        while bit < nctx:
            left = work.shape[1] // 2
            work = work.reshape(ndp, left, 2, r, full.shape[1])
            mine = (me // bit) % 2
            keep = lax.dynamic_index_in_dim(work, mine, 2, keepdims=False)
            give = lax.dynamic_index_in_dim(work, 1 - mine, 2, keepdims=False)
            got = flip(give, "ctx", nctx, bit)
            work = (keep.astype(F32) + got.astype(F32)).astype(BF)
            bit *= 2
        return work.reshape(ndp, r, full.shape[1])

    def finish_slices(full):
        got = lax.all_to_all(ctx_sum(full), "dp", 0, 0, tiled=True)
        return jnp.swapaxes(got, 0, 1).reshape(got.shape[1], -1).astype(F32)

    def finish_sum(full):
        got = lax.all_to_all(ctx_sum(full), "dp", 0, 0, tiled=True)
        return jnp.sum(got.astype(F32), axis=0)

    def local(
        layer_input,
        output_grad,
        prefix,
        attn_gain,
        w_query,
        w_key,
        w_value,
        w_out,
        mlp_gain,
        w_gate,
        w_up,
        w_down,
    ):
        seqs, span, width = layer_input.shape
        q_heads = w_query.shape[1] // HD
        kv_heads = w_key.shape[1] // HD
        group = q_heads // kv_heads
        zi = lax.axis_index("dp")
        rows = layer_input.astype(F32).reshape(seqs * span, width)
        grad_low = output_grad.reshape(seqs * span, width)
        grad_rows = grad_low.astype(F32)
        grad_all = gather_dp(grad_low)

        first = lax.axis_index("ctx") * span
        position = (first + jnp.arange(span)).astype(F32)
        frequency = ROPE_BASE ** (-jnp.arange(HD // 2).astype(F32) * 2.0 / HD)
        angle = position[:, None] * frequency[None, :]
        cosine = jnp.cos(angle)[None, :, None, :]
        sine = jnp.sin(angle)[None, :, None, :]
        normed1 = normed(rows, attn_gain).astype(BF)
        query = rotate(
            dot_plain(normed1, w_query).reshape(seqs, span, q_heads, HD), cosine, sine
        ).astype(BF)
        keyed = rotate(
            dot_plain(normed1, w_key).reshape(seqs, span, kv_heads, HD), cosine, sine
        ).astype(BF)
        valued = dot_plain(normed1, w_value).astype(BF).reshape(seqs, span, kv_heads * HD)
        key_all, value_all = (
            lax.all_gather(
                keyed.reshape(seqs, span, kv_heads * HD), "ctx", axis=1, tiled=True
            ),
            lax.all_gather(valued, "ctx", axis=1, tiled=True),
        )
        length = key_all.shape[1]
        key_all = key_all.reshape(seqs, length, kv_heads, HD)
        value_all = value_all.reshape(seqs, length, kv_heads, HD)
        query5 = query.reshape(seqs, span, kv_heads, group, HD)
        query_pos = first + jnp.arange(span)
        key_pos = jnp.arange(length)
        allowed = (key_pos[None, None, :] <= query_pos[None, :, None]) | (
            key_pos[None, None, :] < prefix[:, None, None]
        )
        scores = score_block(query5, key_all, allowed)
        top = jnp.max(scores, axis=-1, keepdims=True)
        exponent = jnp.exp(scores - top)
        total = jnp.sum(exponent, axis=-1, keepdims=True)
        log_total = top + jnp.log(total)
        probs_low = (exponent / total).astype(BF)
        attended = jnp.einsum(
            "sngcl,slnd->scngd", probs_low, value_all, preferred_element_type=F32
        )
        attended = attended.astype(BF).reshape(seqs * span, q_heads * HD)
        resid = rows + tensor_sum(dot_plain(attended, w_out))
        normed2 = normed(resid, mlp_gain).astype(BF)
        normed2_all = gather_dp(normed2)
        gate = dot_plain(normed2, w_gate)
        up = dot_plain(normed2, w_up)
        act = (jax.nn.silu(gate) * up).astype(BF)

        def mlp_back(gate, up, d_act):
            sigmoid_gate = jax.nn.sigmoid(gate)
            d_gate_pre = (
                d_act * up * sigmoid_gate * (1.0 + gate * (1.0 - sigmoid_gate))
            ).astype(BF)
            d_up_pre = (d_act * gate * sigmoid_gate).astype(BF)
            return d_gate_pre, d_up_pre

        d_act = dot_right(grad_low, w_down)
        d_gate_pre, d_up_pre = mlp_back(gate, up, d_act)
        back_terms = dot_right(d_gate_pre, w_gate) + dot_right(d_up_pre, w_up)
        d_normed2 = tensor_sum(back_terms)
        output = (resid + tensor_sum(dot_plain(act, w_down))).astype(BF)
        output = output.reshape(seqs, span, width)

        units = w_gate.shape[1] // ndp
        wg = lax.dynamic_slice_in_dim(w_gate, zi * units, units, 1)
        wu = lax.dynamic_slice_in_dim(w_up, zi * units, units, 1)
        wd = lax.dynamic_slice_in_dim(w_down, zi * units, units, 0)
        gate_s = dot_plain(normed2_all, wg)
        up_s = dot_plain(normed2_all, wu)
        d_act_s = dot_right(grad_all, wd)
        act_s = (jax.nn.silu(gate_s) * up_s).astype(BF)
        d_gate_s, d_up_s = mlp_back(gate_s, up_s, d_act_s)
        s_down = finish_slices(dot_left(grad_all, act_s).astype(BF)).T
        s_gate = finish_slices(dot_left(normed2_all, d_gate_s).astype(BF))
        s_up = finish_slices(dot_left(normed2_all, d_up_s).astype(BF))

        d_resid_norm, g_mlp_gain = norm_back(resid, mlp_gain, d_normed2)
        d_resid = grad_rows + d_resid_norm
        d_resid_low = d_resid.astype(BF)
        s_out = finish_sum(dot_left(d_resid_low, attended).astype(BF)).T
        d_attended = dot_right(d_resid_low, w_out).astype(BF).reshape(query5.shape)
        scores = score_block(query5, key_all, allowed)
        probs = jnp.exp(scores - log_total)
        probs_low = probs.astype(BF)
        d_probs = jnp.einsum(
            "scngd,slnd->sngcl", d_attended, value_all, preferred_element_type=F32
        )
        delta = jnp.sum(probs * d_probs, axis=-1, keepdims=True)
        d_scores = (probs * (d_probs - delta)).astype(BF)
        scale = HD ** (-0.5)
        d_query = (
            jnp.einsum("sngcl,slnd->scngd", d_scores, key_all, preferred_element_type=F32) * scale
        )
        d_key_all = (
            jnp.einsum("sngcl,scngd->slnd", d_scores, query5, preferred_element_type=F32) * scale
        )
        d_value_all = jnp.einsum(
            "sngcl,scngd->slnd", probs_low, d_attended, preferred_element_type=F32
        )
        d_kv = jnp.concatenate(
            [
                d_key_all.reshape(length, kv_heads * HD).astype(BF),
                d_value_all.reshape(length, kv_heads * HD).astype(BF),
            ],
            axis=1,
        )
        d_kv = lax.psum_scatter(d_kv, "ctx", scatter_dimension=0, tiled=True).astype(F32)
        d_key, d_val = d_kv[:, : kv_heads * HD], d_kv[:, kv_heads * HD :]
        d_qp = (
            rotate_back(d_query.reshape(seqs, span, q_heads, HD), cosine, sine)
            .astype(BF)
            .reshape(seqs * span, q_heads * HD)
        )
        d_kp = (
            rotate_back(d_key.reshape(seqs, span, kv_heads, HD), cosine, sine)
            .astype(BF)
            .reshape(seqs * span, kv_heads * HD)
        )
        d_vp = d_val.astype(BF).reshape(seqs * span, kv_heads * HD)
        front_terms = dot_right(d_qp, w_query) + dot_right(d_kp, w_key) + dot_right(d_vp, w_value)
        d_normed1 = tensor_sum(front_terms)
        d_rows_norm, g_attn_gain = norm_back(rows, attn_gain, d_normed1)
        d_input = d_resid + d_rows_norm
        d_input = d_input.reshape(seqs, span, width)
        s_qkv = finish_sum(
            dot_left(normed1, jnp.concatenate([d_qp, d_kp, d_vp], axis=1)).astype(BF)
        )
        nq, nk = q_heads * HD, kv_heads * HD
        s_query, s_key, s_value = s_qkv[:, :nq], s_qkv[:, nq : nq + nk], s_qkv[:, nq + nk :]
        gains = jnp.stack([g_attn_gain, g_mlp_gain])
        gains = lax.psum_scatter(gains, ("dp", "ctx"), scatter_dimension=1, tiled=True)
        return (
            output,
            d_input,
            gains[0],
            s_query,
            s_key,
            s_value,
            s_out,
            gains[1],
            s_gate,
            s_up,
            s_down,
        )

    return local


def solution(mesh):
    sizes = mesh.shape
    return jax.shard_map(
        build(sizes["dp"], sizes["ctx"], sizes["tensor"]),
        mesh=mesh,
        in_specs=(
            P("dp", "ctx", None),
            P("dp", "ctx", None),
            P("dp"),
            P(),
            P(None, "tensor"),
            P(None, "tensor"),
            P(None, "tensor"),
            P("tensor", None),
            P(),
            P(None, "tensor"),
            P(None, "tensor"),
            P("tensor", None),
        ),
        out_specs=(
            P("dp", "ctx", None),
            P("dp", "ctx", None),
            P(("dp", "ctx")),
            P(("dp", "ctx"), "tensor"),
            P(("dp", "ctx"), "tensor"),
            P(("dp", "ctx"), "tensor"),
            P("tensor", ("dp", "ctx")),
            P(("dp", "ctx")),
            P(("dp", "ctx"), "tensor"),
            P(("dp", "ctx"), "tensor"),
            P("tensor", ("dp", "ctx")),
        ),
        check_vma=False,
    )
```

time: 1200 us -> 585 us (0.49)
  waiting for transfers between devices: 861 us -> 170 us
  starting transfers between devices: 1.81 us -> 52.9 us
  blocking collectives: 40.9 us -> 16.2 us
  local copies, waits for them, and re-layouts: 46.1 us -> 65.6 us
  other arithmetic: 49.5 us -> 67.6 us
  matrix products: 175 us -> 188 us
    reduce_scatter x7 -> x1, waiting for transfers between devices: 472 us -> 0.01 us  [local(): lax.psum_scatter(d_kv, 'ctx', scatter_dimension=0, tiled=True).astype(F32)]
    psum x3 -> x0, waiting for transfers between devices: 169 us -> none  [the longest x1 66.3 us: forward(): lax.psum(dot_plain(act, w_down).astype(jnp.bfloat16), 'tensor')]
    unnamed x14 -> x3, waiting for transfers between devices: 220 us -> 58.1 us
    ppermute x0 -> x26, waiting for transfers between devices: none -> 109 us  [the longest x14 92.5 us: flip(): return lax.ppermute(v, axis, [(i, i ^ bit) for i in range(n)])]
    ppermute x0 -> x26, starting transfers between devices: none -> 28.8 us  [the longest x14 16.8 us: flip(): return lax.ppermute(v, axis, [(i, i ^ bit) for i in range(n)])]
    unnamed x1 -> x0, blocking collectives: 26 us -> none
    all_to_all x0 -> x5, starting transfers between devices: none -> 23.9 us  [the longest x3 14.6 us: finish_slices(): got = lax.all_to_all(ctx_sum(full), 'dp', 0, 0, tiled=True)]
    dot_general x9 -> x11, matrix products: 50.8 us -> 73.1 us  [the longest x9 58.3 us: dot_plain(): return jnp.dot(left, right, preferred_element_type=F32)]
  transfers between devices with their start and end apart: 12 -> 33, of which waited for: 11 -> 10; matrix products, arithmetic and copies ran while one was open for 12% -> 47% of each run, Pallas kernels for 0% -> 0%
where the time goes in v1:
time: 585 us; the launch traced here: 576 us
  matrix products  188 us (32%)
  waiting for transfers between devices  170 us (29%)
  other arithmetic  67.6 us (12%)
  local copies, waits for them, and re-layouts  65.6 us (11%)
  starting transfers between devices  52.9 us (9%)
  blocking collectives  16.2 us (3%)
  between operations  16.1 us (3%)
    ppermute x14, waiting for transfers between devices, flip(): return lax.ppermute(v, axis, [(i, i ^ bit) for i in range(n)])  92.5 us
    dot_general x9, matrix products, dot_plain(): return jnp.dot(left, right, preferred_element_type=F32)  58.3 us
    unnamed x3, waiting for transfers between devices  58.1 us
    dot_general x8, matrix products, dot_right(): lax.dot_general(left, right, (((1,), (1,)), ((), ())), preferred_element_...  53.2 us
    unnamed x147, local copies, waits for them, and re-layouts  33.9 us
    dot_general x5, matrix products, dot_left(): lax.dot_general(left, right, (((0,), (0,)), ((), ())), preferred_element_...  33.6 us
    convert_element_type x5, other arithmetic, ctx_sum(): work = (keep.astype(F32) + got.astype(F32)).astype(BF)  17.1 us
    ppermute x14, starting transfers between devices, flip(): return lax.ppermute(v, axis, [(i, i ^ bit) for i in range(n)])  16.8 us
  transfers between devices with their start and end apart: 33, of which 10 were waited for; matrix products, arithmetic and copies ran while one was open for 47% of the time, Pallas kernels for 0%

profile of v1, /device:TPU:25, one launch (start us, length us, event | category | flops | bytes accessed | tf_op | source)
XLA Modules:
  0.0 575.5 jit_solution(16229616995724655871)
XLA Ops:
  15.8 8.7 %all-gather = bf16[1024,256]{1,0:T(8,128)(2,1)} all-gather(bf16[256,256]{1,0:T(8,128)(2,1)S(1)} %convolution_convert_fusion.8), channel_id=2, replica_groups=mesh['dp'=4,'ctx'=4,'tensor'=2] {'ctx'}, dimensions={0}, use_global_device_ids=true | all-gather | bytes 655360 | tf_op jit(solution)/shard_map/all_gather | solution.py:154
  30.1 7.5 %all_gather.7 = bf16[1,1024,256]{1,2,0:T(8,128)(2,1)S(1)} all-gather(bf16[1,256,256]{1,2,0:T(8,128)(2,1)S(1)} %bitcast.283), channel_id=1, replica_groups=mesh['dp'=4,'ctx'=4,'tensor'=2] {'ctx'}, dimensions={1}, use_global_device_ids=true | all-gather | bytes 655360 | tf_op jit(solution)/shard_map/all_gather | solution.py:151
  37.6 6.7 %copy.49 = bf16[2048,1024]{0,1:T(8,128)(2,1)} copy(bf16[2048,1024]{1,0:T(8,128)(2,1)} %param.16) | data formatting | bytes 8388608 | tf_op args[4]
  49.0 7.2 %fusion.101 = (f32[4,4,256]{2,1,0:T(4,128)S(1)}, f32[1,4,4,256,1024]{3,4,2,1,0:T(8,128)}) fusion(bf16[1024,4,64,1]{0,2,3,1:T(8,128)(2,1)S(1)} %bitcast.253, bf16[256,4,4,32]{0,3,2,1:T(8,128)(2,1)S(1)} %bitcast.266, bf16[256,4,4,32]{0,3,2,1:T(8,128)(2,1)S(1)} %bitcast.264, pred[256,1024]{0,1:T(8,128)(4,1)S(1)} %fusion.71), kind=kOutput, calls=%fused_computation.198 | convolution fusion | flops 550498304 | bytes 18104320 | tf_op jit(solution)/shard_map/scngd,slnd->sngcl/dot_general | solution.py:58
  56.2 8.0 %fusion.3 = f32[4,4,256]{2,1,0:T(4,128)S(1)} fusion(f32[1,4,4,256,1024]{3,4,2,1,0:T(8,128)} %get-tuple-element.51, f32[4,4,256]{2,1,0:T(4,128)S(1)} %get-tuple-element.50), kind=kLoop, calls=%fused_computation.9 | loop fusion | flops 8384512 | bytes 16809984 | tf_op jit(solution)/shard_map/reduce_sum | solution.py:168
  64.3 7.5 %fusion.60 = bf16[4,64,4,256]{3,1,2,0:T(8,128)(2,1)S(1)} fusion(bf16[1024,4,64,1]{0,2,3,1:T(8,128)(2,1)S(1)} %bitcast.269, f32[4,4,256]{2,1,0:T(4,128)S(1)} %fusion.3, f32[1,4,4,256,1024]{3,4,2,1,0:T(8,128)} %get-tuple-element.51, f32[4,4,256]{2,1,0:T(4,128)S(1)} %get-tuple-element.50), kind=kOutput, calls=%fused_computation.114 | convolution fusion | flops 549715968 | bytes 17858560 | tf_op jit(solution)/shard_map/sngcl,slnd->scngd/dot_general | solution.py:171
  76.1 10.2 %fusion.69 = f32[256,4096]{1,0:T(8,128)} fusion(bf16[4096,2048]{1,0:T(8,128)(2,1)} %param.23, bf16[1,256,2048]{2,1,0:T(8,128)(2,1)S(1)} %copy-done.12), kind=kOutput, calls=%fused_computation.125 | convolution fusion | flops 4294967296 | bytes 22020096 | tf_op jit(solution)/shard_map/dot_general | solution.py:21
  91.3 8.4 %collective-permute-done = bf16[256,2048]{1,0:T(8,128)(2,1)} collective-permute-done((bf16[256,2048]{1,0:T(8,128)(2,1)}, bf16[256,2048]{1,0:T(8,128)(2,1)}, u32[]{:S(2)}, u32[]{:S(2)}) %collective-permute-start) | collective-permute-done | bytes 1048608 | tf_op jit(solution)/shard_map/ppermute | solution.py:69
  103.1 11.2 %fusion.102 = f32[256,4096]{1,0:T(8,128)} fusion(bf16[256,2048]{1,0:T(8,128)(2,1)S(1)} %get-tuple-element.27, bf16[2048,4096]{1,0:T(8,128)(2,1)} %param.21), kind=kOutput, calls=%fused_computation.199 | convolution fusion | flops 4294967296 | bytes 22020096 | tf_op jit(solution)/shard_map/dot_general | solution.py:17
  114.4 6.3 %fusion.103 = f32[256,4096]{1,0:T(8,128)} fusion(bf16[256,2048]{1,0:T(8,128)(2,1)S(1)} %get-tuple-element.27, bf16[2048,4096]{1,0:T(8,128)(2,1)S(1)} %bitcast.296), kind=kOutput, calls=%fused_computation.200 | convolution fusion | flops 4294967296 | bytes 22020096 | tf_op jit(solution)/shard_map/dot_general | solution.py:17
  120.7 13.9 %fusion.42 = f32[256,2048]{1,0:T(8,128)} fusion(bf16[2048,4096]{1,0:T(8,128)(2,1)} %param.21, f32[256,4096]{1,0:T(8,128)} %fusion.102, f32[256,4096]{1,0:T(8,128)} %fusion.69, f32[256,4096]{1,0:T(8,128)} %fusion.103), kind=kOutput, calls=%fused_computation.75 | convolution fusion | flops 4305453056 | bytes 31457280 | tf_op jit(solution)/shard_map/dot_general | solution.py:21
  134.5 11.1 %fusion.30 = bf16[256,2048]{1,0:T(8,128)(2,1)S(1)} fusion(f32[256,2048]{1,0:T(8,128)} %fusion.42, bf16[2048,4096]{1,0:T(8,128)(2,1)} %param.22, f32[256,4096]{1,0:T(8,128)} %fusion.69, f32[256,4096]{1,0:T(8,128)} %fusion.102), kind=kOutput, calls=%fused_computation.61 | convolution fusion | flops 4302307328 | bytes 28311552 | tf_op jit(solution)/shard_map/dot_general | solution.py:21
  145.6 13.0 %convolution_convert_fusion.5 = bf16[256,2048]{1,0:T(8,128)(2,1)S(1)} fusion(bf16[4096,2048]{1,0:T(8,128)(2,1)} %param.23, f32[256,4096]{1,0:T(8,128)} %fusion.103, f32[256,4096]{1,0:T(8,128)} %fusion.102), kind=kOutput, calls=%fused_computation.62 | convolution fusion | flops 4301783040 | bytes 26214400 | tf_op jit(solution)/shard_map/dot_general | solution.py:17
  167.8 9.9 %fusion.21 = f32[1024,1024]{1,0:T(8,128)} fusion(bf16[1024,2048]{1,0:T(8,128)(2,1)S(1)} %constant_dynamic-update-slice_fusion.7, bf16[4096,2048]{1,0:T(8,128)(2,1)} %param.23, s32[]{:T(128)S(6)} %select_n.95), kind=kOutput, calls=%fused_computation.36 | convolution fusion | flops 4294967296 | bytes 12582916 | tf_op jit(solution)/shard_map/dot_general | solution.py:21
  179.1 16.7 %collective-permute-done.10 = bf16[128,2048]{1,0:T(8,128)(2,1)} collective-permute-done((bf16[128,2048]{1,0:T(8,128)(2,1)S(1)}, bf16[128,2048]{1,0:T(8,128)(2,1)}, u32[]{:S(2)}, u32[]{:S(2)}) %collective-permute-start.10) | collective-permute-done | bytes 524320 | tf_op jit(solution)/shard_map/ppermute | solution.py:66
  200.0 9.9 %collective-permute-done.1 = bf16[256,2048]{1,0:T(8,128)(2,1)S(1)} collective-permute-done((bf16[256,2048]{1,0:T(8,128)(2,1)S(1)}, bf16[256,2048]{1,0:T(8,128)(2,1)S(1)}, u32[]{:S(2)}, u32[]{:S(2)}) %collective-permute-start.1) | collective-permute-done | bytes 1048608 | tf_op jit(solution)/shard_map/ppermute | solution.py:69
  216.5 15.0 %fusion = (f32[4,4,256]{2,1,0:T(4,128)S(1)}, f32[4,1024,256,4]{2,1,3,0:T(8,128)}) fusion(f32[1,4,4,256,1024]{3,4,2,1,0:T(8,128)} %get-tuple-element.51, f32[4,4,256]{2,1,0:T(4,128)S(1)} %bitcast.285, bf16[1024,4,64,1]{0,2,3,1:T(8,128)(2,1)} %bitcast.268, bf16[256,4,4,64]{0,3,2,1:T(8,128)(2,1)} %bitcast.251), kind=kOutput, calls=%fused_computation.3 | convolution fusion | flops 549449728 | bytes 34635776 | tf_op jit(solution)/shard_map/scngd,slnd->sngcl/dot_general | solution.py:218
  231.5 8.6 %fusion.56 = bf16[4,64,1024]{2,1,0:T(8,128)(2,1)S(1)} fusion(bf16[256,4,4,64]{0,3,2,1:T(8,128)(2,1)S(1)} %bitcast.252, f32[1,4,4,256,1024]{3,4,2,1,0:T(8,128)} %get-tuple-element.51, f32[4,4,256]{2,1,0:T(4,128)S(1)} %bitcast.286), kind=kOutput, calls=%fused_computation.111 | convolution fusion | flops 545521664 | bytes 17842176 | tf_op jit(solution)/shard_map/sngcl,scngd->slnd/dot_general | solution.py:230
  249.0 10.2 %fusion.17 = f32[1024,1024]{1,0:T(8,128)} fusion(bf16[1024,2048]{1,0:T(8,128)(2,1)S(1)} %constant_dynamic-update-slice_fusion, bf16[2048,4096]{1,0:T(8,128)(2,1)} %param.21, s32[]{:T(128)S(6)} %select_n.95), kind=kOutput, calls=%fused_computation.32 | convolution fusion | flops 4294967296 | bytes 12582916 | tf_op jit(solution)/shard_map/dot_general | solution.py:17
  259.1 8.4 %fusion.19 = f32[1024,1024]{1,0:T(8,128)} fusion(bf16[1024,2048]{1,0:T(8,128)(2,1)S(1)} %constant_dynamic-update-slice_fusion, bf16[2048,4096]{1,0:T(8,128)(2,1)} %param.22, s32[]{:T(128)S(6)} %select_n.95), kind=kOutput, calls=%fused_computation.34 | convolution fusion | flops 4294967296 | bytes 12582916 | tf_op jit(solution)/shard_map/dot_general | solution.py:17
  267.6 8.0 %fusion.8 = bf16[4,4,256,1024]{2,3,1,0:T(8,128)(2,1)S(1)} fusion(f32[4,1024,256,4]{2,1,3,0:T(8,128)} %get-tuple-element.53, f32[1,4,4,256,1024]{3,4,2,1,0:T(8,128)S(1)} %bitcast.245, f32[4,4,256]{2,1,0:T(4,128)S(1)} %get-tuple-element.52, f32[4,4,256]{2,1,0:T(4,128)S(1)} %bitcast.287), kind=kLoop, calls=%fused_computation.13 | loop fusion | flops 16777216 | bytes 41975808 | tf_op jit(solution)/shard_map/reshape.27
  285.8 6.2 %collective-permute-start.6 = (bf16[4,2,128,1024]{3,2,0,1:T(8,128)(2,1)}, bf16[4,2,128,1024]{3,2,0,1:T(8,128)(2,1)S(1)}, u32[]{:S(2)}, u32[]{:S(2)}) collective-permute-start(bf16[4,2,128,1024]{3,2,0,1:T(8,128)(2,1)} %bitcast.239), channel_id=1, source_target_pairs={{0,2},{2,0},{4,6},{6,4},{1,3},{3,1},{5,7},{7,5},{8,10},{10,8},{12,... | collective-permute-start | bytes 6291464 | tf_op jit(solution)/shard_map/ppermute | solution.py:69
  292.0 5.2 convolution_convert_fusion.3
  297.3 12.2 %convolution_convert_fusion.4 = bf16[2048,1024]{1,0:T(8,128)(2,1)S(1)} fusion(bf16[1024,2048]{1,0:T(8,128)(2,1)S(1)} %copy-done.42, f32[1024,1024]{1,0:T(8,128)} %fusion.17, f32[1024,1024]{1,0:T(8,128)} %fusion.21, f32[1024,1024]{1,0:T(8,128)} %fusion.19), kind=kOutput, calls=%fused_computation.45 | convolution fusion | flops 4307550208 | bytes 20971520 | tf_op jit(solution)/shard_map/dot_general | solution.py:25
  309.5 10.9 %convolution_convert_fusion.2 = bf16[2048,1024]{1,0:T(8,128)(2,1)S(1)} fusion(bf16[1024,2048]{1,0:T(8,128)(2,1)} %copy-done.45, f32[1024,1024]{1,0:T(8,128)} %fusion.19, f32[1024,1024]{1,0:T(8,128)} %fusion.17), kind=kOutput, calls=%fused_computation.43 | convolution fusion | flops 4303355904 | bytes 16777216 | tf_op jit(solution)/shard_map/dot_general | solution.py:25
  343.6 17.1 %collective-permute-done.7 = bf16[4,1,128,1024]{3,2,0,1:T(8,128)(2,1)S(1)} collective-permute-done((bf16[4,1,128,1024]{3,2,0,1:T(8,128)(2,1)S(1)}, bf16[4,1,128,1024]{3,2,0,1:T(8,128)(2,1)S(1)}, u32[]{:S(2)}, u32[]{:S(2)}) %collective-permute-start.7) | collective-permute-done | bytes 1048608 | tf_op jit(solution)/shard_map/ppermute | solution.py:69
  374.9 18.8 %collective-permute-done.21 = bf16[4,1,128,1024]{3,2,1,0:T(8,128)(2,1)S(1)} collective-permute-done((bf16[4,1,128,1024]{3,2,1,0:T(8,128)(2,1)S(1)}, bf16[4,1,128,1024]{3,2,1,0:T(8,128)(2,1)S(1)}, u32[]{:S(2)}, u32[]{:S(2)}) %collective-permute-start.21) | collective-permute-done | bytes 1048608 | tf_op jit(solution)/shard_map/ppermute | solution.py:69
  414.2 9.8 %collective-permute-done.23 = bf16[4,1,128,1024]{3,2,1,0:T(8,128)(2,1)S(1)} collective-permute-done((bf16[4,1,128,1024]{3,2,1,0:T(8,128)(2,1)S(1)}, bf16[4,1,128,1024]{3,2,1,0:T(8,128)(2,1)S(1)}, u32[]{:S(2)}, u32[]{:S(2)}) %collective-permute-start.23) | collective-permute-done | bytes 1048608 | tf_op jit(solution)/shard_map/ppermute | solution.py:69
  439.3 7.2 %collective-permute-done.25 = bf16[4,1,128,1024]{3,2,1,0:T(8,128)(2,1)} collective-permute-done((bf16[4,1,128,1024]{3,2,1,0:T(8,128)(2,1)}, bf16[4,1,128,1024]{3,2,1,0:T(8,128)(2,1)}, u32[]{:S(2)}, u32[]{:S(2)}) %collective-permute-start.25) | collective-permute-done | bytes 1048608 | tf_op jit(solution)/shard_map/ppermute | solution.py:69
  451.2 5.3 all-to-all-start.4
  458.8 21.4 %collective-permute-done.5 = bf16[4,1,128,1536]{3,2,1,0:T(8,128)(2,1)} collective-permute-done((bf16[4,1,128,1536]{3,2,1,0:T(8,128)(2,1)}, bf16[4,1,128,1536]{3,2,1,0:T(8,128)(2,1)}, u32[]{:S(2)}, u32[]{:S(2)}) %collective-permute-start.5) | collective-permute-done | bytes 1572896 | tf_op jit(solution)/shard_map/ppermute | solution.py:69
  493.3 58.1 %reduce-scatter.7.cloned.1.call-done = f32[128,2]{1,0:T(8,128)} async-done(((f32[2048,2]{1,0:T(8,128)}), f32[128,2]{1,0:T(8,128)}) %reduce-scatter.7.cloned.1.call-update) | async-done | bytes 1040
  (285 shorter events, 180.9 us)
Async XLA Ops:
  7.2 323.0 %reduce-scatter.5.cloned.1.call-start = ((), (), s32[]{:S(2)}) async-start(), calls=%async_computation.7 | async-start | bytes 1310720 | tf_op jit(solution)/shard_map/reduce_scatter | solution.py:240
  9.3 77.2 %collective-permute-start.14 = (bf16[128,2048]{1,0:T(8,128)(2,1)}, bf16[128,2048]{1,0:T(8,128)(2,1)}, u32[]{:S(2)}, u32[]{:S(2)}) collective-permute-start(bf16[128,2048]{1,0:T(8,128)(2,1)} %dynamic-slice_bitcast_fusion.4), channel_id=1, source_target_pairs={{8,0},{16,8},{24,16},{0,24},{9,1},{17,9},{25,17},{1,25},{10,2},{18... | collective-permute-start | bytes 1572872 | tf_op jit(solution)/shard_map/ppermute | solution.py:66
  9.4 77.3 %collective-permute-start.16 = (bf16[128,2048]{1,0:T(8,128)(2,1)}, bf16[128,2048]{1,0:T(8,128)(2,1)}, u32[]{:S(2)}, u32[]{:S(2)}) collective-permute-start(bf16[128,2048]{1,0:T(8,128)(2,1)} %dynamic-slice_bitcast_fusion.4), channel_id=1, source_target_pairs={{16,0},{24,8},{0,16},{8,24},{17,1},{25,9},{1,17},{9,25},{18,2},{26... | collective-permute-start | bytes 1572872 | tf_op jit(solution)/shard_map/ppermute | solution.py:66
  9.5 78.6 %collective-permute-start.18 = (bf16[128,2048]{1,0:T(8,128)(2,1)}, bf16[128,2048]{1,0:T(8,128)(2,1)}, u32[]{:S(2)}, u32[]{:S(2)}) collective-permute-start(bf16[128,2048]{1,0:T(8,128)(2,1)} %dynamic-slice_bitcast_fusion.4), channel_id=1, source_target_pairs={{24,0},{0,8},{8,16},{16,24},{25,1},{1,9},{9,17},{17,25},{26,2},{2,... | collective-permute-start | bytes 1572872 | tf_op jit(solution)/shard_map/ppermute | solution.py:66
  74.9 24.9 %collective-permute-start = (bf16[256,2048]{1,0:T(8,128)(2,1)}, bf16[256,2048]{1,0:T(8,128)(2,1)}, u32[]{:S(2)}, u32[]{:S(2)}) collective-permute-start(bf16[256,2048]{1,0:T(8,128)(2,1)} %convolution_convert_fusion.6), channel_id=1, source_target_pairs={{0,1},{1,0},{2,3},{3,2},{4,5},{5,4},{6,7},{7,6},{8,9},{9,8},{10,11... | collective-permute-start | bytes 3145736 | tf_op jit(solution)/shard_map/ppermute | solution.py:69
  86.5 74.1 %collective-permute-start.15 = (bf16[128,2048]{1,0:T(8,128)(2,1)}, bf16[128,2048]{1,0:T(8,128)(2,1)}, u32[]{:S(2)}, u32[]{:S(2)}) collective-permute-start(bf16[128,2048]{1,0:T(8,128)(2,1)} %collective-permute-done.14), channel_id=1, source_target_pairs={{1,0},{0,1},{3,2},{2,3},{5,4},{4,5},{7,6},{6,7},{9,8},{8,9},{11,10... | collective-permute-start | bytes 1572872 | tf_op jit(solution)/shard_map/ppermute | solution.py:66
  86.8 78.3 %collective-permute-start.17 = (bf16[128,2048]{1,0:T(8,128)(2,1)}, bf16[128,2048]{1,0:T(8,128)(2,1)S(1)}, u32[]{:S(2)}, u32[]{:S(2)}) collective-permute-start(bf16[128,2048]{1,0:T(8,128)(2,1)} %collective-permute-done.16), channel_id=1, source_target_pairs={{1,0},{0,1},{3,2},{2,3},{5,4},{4,5},{7,6},{6,7},{9,8},{8,9},{11,10... | collective-permute-start | bytes 1572872 | tf_op jit(solution)/shard_map/ppermute | solution.py:66
  88.0 79.5 %collective-permute-start.19 = (bf16[128,2048]{1,0:T(8,128)(2,1)}, bf16[128,2048]{1,0:T(8,128)(2,1)S(1)}, u32[]{:S(2)}, u32[]{:S(2)}) collective-permute-start(bf16[128,2048]{1,0:T(8,128)(2,1)} %collective-permute-done.18), channel_id=1, source_target_pairs={{1,0},{0,1},{3,2},{2,3},{5,4},{4,5},{7,6},{6,7},{9,8},{8,9},{11,10... | collective-permute-start | bytes 1572872 | tf_op jit(solution)/shard_map/ppermute | solution.py:66
  158.7 19.1 %collective-permute-start.8 = (bf16[128,2048]{1,0:T(8,128)(2,1)S(1)}, bf16[128,2048]{1,0:T(8,128)(2,1)}, u32[]{:S(2)}, u32[]{:S(2)}) collective-permute-start(bf16[128,2048]{1,0:T(8,128)(2,1)S(1)} %constant_dynamic-slice_fusion.3), channel_id=1, source_target_pairs={{8,0},{16,8},{24,16},{0,24},{9,1},{17,9},{25,17},{1,25},{10,2},{18... | collective-permute-start | bytes 1572872 | tf_op jit(solution)/shard_map/ppermute | solution.py:66
  159.0 36.8 %collective-permute-start.10 = (bf16[128,2048]{1,0:T(8,128)(2,1)S(1)}, bf16[128,2048]{1,0:T(8,128)(2,1)}, u32[]{:S(2)}, u32[]{:S(2)}) collective-permute-start(bf16[128,2048]{1,0:T(8,128)(2,1)S(1)} %constant_dynamic-slice_fusion.3), channel_id=1, source_target_pairs={{16,0},{24,8},{0,16},{8,24},{17,1},{25,9},{1,17},{9,25},{18,2},{26... | collective-permute-start | bytes 1572872 | tf_op jit(solution)/shard_map/ppermute | solution.py:66
  160.6 36.5 %collective-permute-start.12 = (bf16[128,2048]{1,0:T(8,128)(2,1)S(1)}, bf16[128,2048]{1,0:T(8,128)(2,1)}, u32[]{:S(2)}, u32[]{:S(2)}) collective-permute-start(bf16[128,2048]{1,0:T(8,128)(2,1)S(1)} %constant_dynamic-slice_fusion.3), channel_id=1, source_target_pairs={{24,0},{0,8},{8,16},{16,24},{25,1},{1,9},{9,17},{17,25},{26,2},{2,... | collective-permute-start | bytes 1572872 | tf_op jit(solution)/shard_map/ppermute | solution.py:66
  165.0 34.1 %collective-permute-start.2 = (bf16[256,2048]{1,0:T(8,128)(2,1)S(1)}, bf16[256,2048]{1,0:T(8,128)(2,1)S(1)}, u32[]{:S(2)}, u32[]{:S(2)}) collective-permute-start(bf16[256,2048]{1,0:T(8,128)(2,1)S(1)} %fusion.30), channel_id=1, source_target_pairs={{0,1},{1,0},{2,3},{3,2},{4,5},{5,4},{6,7},{7,6},{8,9},{9,8},{10,11... | collective-permute-start | bytes 3145736 | tf_op jit(solution)/shard_map/ppermute | solution.py:69
  167.5 42.3 %collective-permute-start.1 = (bf16[256,2048]{1,0:T(8,128)(2,1)S(1)}, bf16[256,2048]{1,0:T(8,128)(2,1)S(1)}, u32[]{:S(2)}, u32[]{:S(2)}) collective-permute-start(bf16[256,2048]{1,0:T(8,128)(2,1)S(1)} %convolution_convert_fusion.5), channel_id=1, source_target_pairs={{0,1},{1,0},{2,3},{3,2},{4,5},{5,4},{6,7},{7,6},{8,9},{9,8},{10,11... | collective-permute-start | bytes 3145736 | tf_op jit(solution)/shard_map/ppermute | solution.py:69
  177.8 62.3 %collective-permute-start.9 = (bf16[128,2048]{1,0:T(8,128)(2,1)}, bf16[128,2048]{1,0:T(8,128)(2,1)}, u32[]{:S(2)}, u32[]{:S(2)}) collective-permute-start(bf16[128,2048]{1,0:T(8,128)(2,1)} %collective-permute-done.8), channel_id=1, source_target_pairs={{1,0},{0,1},{3,2},{2,3},{5,4},{4,5},{7,6},{6,7},{9,8},{8,9},{11,10... | collective-permute-start | bytes 1572872 | tf_op jit(solution)/shard_map/ppermute | solution.py:66
  195.8 46.6 %collective-permute-start.11 = (bf16[128,2048]{1,0:T(8,128)(2,1)}, bf16[128,2048]{1,0:T(8,128)(2,1)}, u32[]{:S(2)}, u32[]{:S(2)}) collective-permute-start(bf16[128,2048]{1,0:T(8,128)(2,1)} %collective-permute-done.10), channel_id=1, source_target_pairs={{1,0},{0,1},{3,2},{2,3},{5,4},{4,5},{7,6},{6,7},{9,8},{8,9},{11,10... | collective-permute-start | bytes 1572872 | tf_op jit(solution)/shard_map/ppermute | solution.py:66
  197.0 50.8 %collective-permute-start.13 = (bf16[128,2048]{1,0:T(8,128)(2,1)}, bf16[128,2048]{1,0:T(8,128)(2,1)}, u32[]{:S(2)}, u32[]{:S(2)}) collective-permute-start(bf16[128,2048]{1,0:T(8,128)(2,1)} %collective-permute-done.12), channel_id=1, source_target_pairs={{1,0},{0,1},{3,2},{2,3},{5,4},{4,5},{7,6},{6,7},{9,8},{8,9},{11,10... | collective-permute-start | bytes 1572872 | tf_op jit(solution)/shard_map/ppermute | solution.py:66
  285.8 45.4 %collective-permute-start.6 = (bf16[4,2,128,1024]{3,2,0,1:T(8,128)(2,1)}, bf16[4,2,128,1024]{3,2,0,1:T(8,128)(2,1)S(1)}, u32[]{:S(2)}, u32[]{:S(2)}) collective-permute-start(bf16[4,2,128,1024]{3,2,0,1:T(8,128)(2,1)} %bitcast.239), channel_id=1, source_target_pairs={{0,2},{2,0},{4,6},{6,4},{1,3},{3,1},{5,7},{7,5},{8,10},{10,8},{12,... | collective-permute-start | bytes 6291464 | tf_op jit(solution)/shard_map/ppermute | solution.py:69
  322.0 44.8 %collective-permute-start.20 = (bf16[4,2,128,1024]{3,2,1,0:T(8,128)(2,1)}, bf16[4,2,128,1024]{3,2,1,0:T(8,128)(2,1)}, u32[]{:S(2)}, u32[]{:S(2)}) collective-permute-start(bf16[4,2,128,1024]{3,2,1,0:T(8,128)(2,1)} %dynamic-slice_bitcast_fusion.3), channel_id=1, source_target_pairs={{0,2},{2,0},{4,6},{6,4},{1,3},{3,1},{5,7},{7,5},{8,10},{10,8},{12,... | collective-permute-start | bytes 6291464 | tf_op jit(solution)/shard_map/ppermute | solution.py:69
  325.5 45.5 %collective-permute-start.22 = (bf16[4,2,128,1024]{3,2,1,0:T(8,128)(2,1)}, bf16[4,2,128,1024]{3,2,1,0:T(8,128)(2,1)}, u32[]{:S(2)}, u32[]{:S(2)}) collective-permute-start(bf16[4,2,128,1024]{3,2,1,0:T(8,128)(2,1)} %dynamic-slice_bitcast_fusion.2), channel_id=1, source_target_pairs={{0,2},{2,0},{4,6},{6,4},{1,3},{3,1},{5,7},{7,5},{8,10},{10,8},{12,... | collective-permute-start | bytes 6291464 | tf_op jit(solution)/shard_map/ppermute | solution.py:69
  327.1 79.3 %collective-permute-start.24 = (bf16[4,2,128,1024]{3,2,1,0:T(8,128)(2,1)}, bf16[4,2,128,1024]{3,2,1,0:T(8,128)(2,1)}, u32[]{:S(2)}, u32[]{:S(2)}) collective-permute-start(bf16[4,2,128,1024]{3,2,1,0:T(8,128)(2,1)} %dynamic-slice_bitcast_fusion.1), channel_id=1, source_target_pairs={{0,2},{2,0},{4,6},{6,4},{1,3},{3,1},{5,7},{7,5},{8,10},{10,8},{12,... | collective-permute-start | bytes 6291464 | tf_op jit(solution)/shard_map/ppermute | solution.py:69
  335.9 24.8 %collective-permute-start.7 = (bf16[4,1,128,1024]{3,2,0,1:T(8,128)(2,1)S(1)}, bf16[4,1,128,1024]{3,2,0,1:T(8,128)(2,1)S(1)}, u32[]{:S(2)}, u32[]{:S(2)}) collective-permute-start(bf16[4,1,128,1024]{3,2,0,1:T(8,128)(2,1)S(1)} %constant_dynamic-slice_fusion.4), channel_id=1, source_target_pairs={{0,4},{2,6},{4,0},{6,2},{1,5},{3,7},{5,1},{7,3},{8,12},{10,14},{12... | collective-permute-start | bytes 3145736 | tf_op jit(solution)/shard_map/ppermute | solution.py:69
  343.3 86.8 %collective-permute-start.4 = (bf16[4,2,128,1536]{3,2,1,0:T(8,128)(2,1)}, bf16[4,2,128,1536]{3,2,1,0:T(8,128)(2,1)}, u32[]{:S(2)}, u32[]{:S(2)}) collective-permute-start(bf16[4,2,128,1536]{3,2,1,0:T(8,128)(2,1)} %dynamic-slice_bitcast_fusion), channel_id=1, source_target_pairs={{0,2},{2,0},{4,6},{6,4},{1,3},{3,1},{5,7},{7,5},{8,10},{10,8},{12,... | collective-permute-start | bytes 9437192 | tf_op jit(solution)/shard_map/ppermute | solution.py:69
  362.1 33.0 %all-to-all-start.1 = ((bf16[4,128,1024]{2,1,0:T(8,128)(2,1)}), bf16[4,128,1024]{2,1,0:T(8,128)(2,1)S(1)}, u32[]{:S(2)}, u32[]{:S(2)}) async-start(bf16[4,128,1024]{2,1,0:T(8,128)(2,1)} %fusion.64), calls=%async_computation.2 | async-start | bytes 2097152 | tf_op jit(solution)/shard_map/all_to_all | solution.py:109
  370.3 23.3 %collective-permute-start.21 = (bf16[4,1,128,1024]{3,2,1,0:T(8,128)(2,1)S(1)}, bf16[4,1,128,1024]{3,2,1,0:T(8,128)(2,1)S(1)}, u32[]{:S(2)}, u32[]{:S(2)}) collective-permute-start(bf16[4,1,128,1024]{3,2,1,0:T(8,128)(2,1)S(1)} %constant_dynamic-slice_fusion.2), channel_id=1, source_target_pairs={{0,4},{2,6},{4,0},{6,2},{1,5},{3,7},{5,1},{7,3},{8,12},{10,14},{12... | collective-permute-start | bytes 3145736 | tf_op jit(solution)/shard_map/ppermute | solution.py:69
  396.0 29.3 %all-to-all-start.2 = ((bf16[4,128,1024]{2,1,0:T(8,128)(2,1)}), bf16[4,128,1024]{2,1,0:T(8,128)(2,1)S(1)}, u32[]{:S(2)}, u32[]{:S(2)}) async-start(bf16[4,128,1024]{2,1,0:T(8,128)(2,1)} %fusion.65), calls=%async_computation.3 | async-start | bytes 2097152 | tf_op jit(solution)/shard_map/all_to_all | solution.py:105
  402.0 21.9 %collective-permute-start.23 = (bf16[4,1,128,1024]{3,2,1,0:T(8,128)(2,1)S(1)}, bf16[4,1,128,1024]{3,2,1,0:T(8,128)(2,1)S(1)}, u32[]{:S(2)}, u32[]{:S(2)}) collective-permute-start(bf16[4,1,128,1024]{3,2,1,0:T(8,128)(2,1)S(1)} %constant_dynamic-slice_fusion.1), channel_id=1, source_target_pairs={{0,4},{2,6},{4,0},{6,2},{1,5},{3,7},{5,1},{7,3},{8,12},{10,14},{12... | collective-permute-start | bytes 3145736 | tf_op jit(solution)/shard_map/ppermute | solution.py:69
  411.5 35.0 %collective-permute-start.25 = (bf16[4,1,128,1024]{3,2,1,0:T(8,128)(2,1)}, bf16[4,1,128,1024]{3,2,1,0:T(8,128)(2,1)}, u32[]{:S(2)}, u32[]{:S(2)}) collective-permute-start(bf16[4,1,128,1024]{3,2,1,0:T(8,128)(2,1)} %constant_dynamic-slice_fusion), channel_id=1, source_target_pairs={{0,4},{2,6},{4,0},{6,2},{1,5},{3,7},{5,1},{7,3},{8,12},{10,14},{12... | collective-permute-start | bytes 3145736 | tf_op jit(solution)/shard_map/ppermute | solution.py:69
  425.4 25.8 %all-to-all-start.3 = ((bf16[4,128,1024]{2,1,0:T(8,128)(2,1)}), bf16[4,128,1024]{2,1,0:T(8,128)(2,1)}, u32[]{:S(2)}, u32[]{:S(2)}) async-start(bf16[4,128,1024]{2,1,0:T(8,128)(2,1)} %fusion.66), calls=%async_computation.4 | async-start | bytes 2097152 | tf_op jit(solution)/shard_map/all_to_all | solution.py:105
  436.8 43.4 %collective-permute-start.5 = (bf16[4,1,128,1536]{3,2,1,0:T(8,128)(2,1)}, bf16[4,1,128,1536]{3,2,1,0:T(8,128)(2,1)}, u32[]{:S(2)}, u32[]{:S(2)}) collective-permute-start(bf16[4,1,128,1536]{3,2,1,0:T(8,128)(2,1)} %constant_dynamic-slice_fusion.7), channel_id=1, source_target_pairs={{0,4},{2,6},{4,0},{6,2},{1,5},{3,7},{5,1},{7,3},{8,12},{10,14},{12... | collective-permute-start | bytes 4718600 | tf_op jit(solution)/shard_map/ppermute | solution.py:69
  451.2 32.0 %all-to-all-start.4 = ((bf16[4,128,1024]{2,1,0:T(8,128)(2,1)}), bf16[4,128,1024]{2,1,0:T(8,128)(2,1)}, u32[]{:S(2)}, u32[]{:S(2)}) async-start(bf16[4,128,1024]{2,1,0:T(8,128)(2,1)} %fusion.67), calls=%async_computation.5 | async-start | bytes 2097152 | tf_op jit(solution)/shard_map/all_to_all | solution.py:105
  483.2 82.0 %all-to-all-start = ((bf16[4,128,1536]{2,1,0:T(8,128)(2,1)}), bf16[4,128,1536]{2,1,0:T(8,128)(2,1)}, u32[]{:S(2)}, u32[]{:S(2)}) async-start(bf16[4,128,1536]{2,1,0:T(8,128)(2,1)} %fusion.51), calls=%async_computation.1 | async-start | bytes 3145728 | tf_op jit(solution)/shard_map/all_to_all | solution.py:109
  487.8 63.6 %reduce-scatter.7.cloned.1.call-start = ((), (), s32[]{:S(2)}) async-start(), calls=%async_computation.8 | async-start | bytes 1114112
  (66 other events, 719.4 us)
Sparse Core Ops, SparseCore 0:
  280.2 30.6 reduce-scatter.4
  492.7 58.5 reduce-scatter.6

commit v2 on v1

--- a/solution.py
+++ b/solution.py
@@ -1,16 +1,479 @@
+import functools
 import jax
 import jax.numpy as jnp
 from jax import lax
+from jax.experimental import pallas as pl
+from jax.experimental.pallas import tpu as pltpu
 from jax.sharding import PartitionSpec as P
 
 HD = 64
-
-
 EPS = 1e-05
 ROPE_BASE = 500000.0
 NEG = -1e30
 BF = jnp.bfloat16
 F32 = jnp.float32
+VMEM_MOST = 60 * 1024 * 1024
+
+
+def cost(flops, nbytes, trans=0):
+    return pl.CostEstimate(flops=int(flops), bytes_accessed=int(nbytes), transcendentals=int(trans))
+
+
+def nt(a, b):
+    return lax.dot_general(a, b, (((1,), (1,)), ((), ())), preferred_element_type=F32)
+
+
+def tn(a, b):
+    return lax.dot_general(a, b, (((0,), (0,)), ((), ())), preferred_element_type=F32)
+
+
+def nn(a, b):
+    return jnp.dot(a, b, preferred_element_type=F32)
+
+
+def swap_halves(t):
+    lane = lax.broadcasted_iota(jnp.int32, t.shape, 1) % HD
+    n = t.shape[1]
+    return jnp.where(
+        lane < HD // 2, pltpu.roll(t, n - HD // 2, 1), pltpu.roll(t, HD // 2, 1)
+    )
+
+
+def rope_tables(first, span):
+    position = (first + jnp.arange(span)).astype(F32)
+    frequency = ROPE_BASE ** (-jnp.arange(HD // 2).astype(F32) * 2.0 / HD)
+    angle = position[:, None] * frequency[None, :]
+    cosine, sine = jnp.cos(angle), jnp.sin(angle)
+    return (
+        jnp.concatenate([cosine, cosine, cosine, cosine], axis=1),
+        jnp.concatenate([-sine, sine, -sine, sine], axis=1),
+    )
+
+
+def qkv_kernel(x_ref, gain_ref, wq_ref, wk_ref, wv_ref, cos_ref, sin_ref, n_ref, q_ref, kv_ref):
+    cosine, sine = cos_ref[...], sin_ref[...]
+
+    def rope(t):
+        pieces = []
+        for i in range(t.shape[1] // 128):
+            part = t[:, 128 * i : 128 * (i + 1)]
+            pieces.append((part * cosine + swap_halves(part) * sine).astype(BF))
+        return pieces
+
+    @pl.when(pl.program_id(0) == 0)
+    def _():
+        v = x_ref[...].astype(F32)
+        factor = lax.rsqrt(jnp.mean(v * v, axis=-1, keepdims=True) + EPS)
+        n_ref[...] = (v * factor * gain_ref[...]).astype(BF)
+        width = wk_ref.shape[1]
+        for i, part in enumerate(rope(nn(n_ref[...], wk_ref[...]))):
+            kv_ref[:, 128 * i : 128 * (i + 1)] = part
+        kv_ref[:, width:] = nn(n_ref[...], wv_ref[...]).astype(BF)
+
+    for i, part in enumerate(rope(nn(n_ref[...], wq_ref[...]))):
+        q_ref[:, 128 * i : 128 * (i + 1)] = part
+
+
+def qkv(x, gain, wq, wk, wv, cosine, sine):
+    rows, width = x.shape
+    step = 256
+    grid = wq.shape[1] // step
+    whole = lambda a: pl.BlockSpec(a.shape, lambda j: (0, 0))
+    kv_width = wk.shape[1] + wv.shape[1]
+    return pl.pallas_call(
+        qkv_kernel,
+        grid=(grid,),
+        in_specs=[
+            whole(x),
+            pl.BlockSpec((1, width), lambda j: (0, 0)),
+            pl.BlockSpec((width, step), lambda j: (0, j)),
+            whole(wk),
+            whole(wv),
+            whole(cosine),
+            whole(sine),
+        ],
+        out_specs=[
+            pl.BlockSpec((rows, width), lambda j: (0, 0)),
+            pl.BlockSpec((rows, step), lambda j: (0, j)),
+            pl.BlockSpec((rows, kv_width), lambda j: (0, 0)),
+        ],
+        out_shape=[
+            jax.ShapeDtypeStruct((rows, width), BF),
+            jax.ShapeDtypeStruct((rows, wq.shape[1]), BF),
+            jax.ShapeDtypeStruct((rows, kv_width), BF),
+        ],
+        compiler_params=pltpu.CompilerParams(vmem_limit_bytes=40 * 1024 * 1024),
+        cost_estimate=cost(
+            2 * rows * width * (wq.shape[1] + kv_width), 2 * width * (wq.shape[1] + kv_width)
+        ),
+        name="qkv",
+    )(x, gain.reshape(1, width), wq, wk, wv, cosine, sine)
+
+
+def mask_bias(first, prefix, length, span):
+    key = lax.broadcasted_iota(jnp.int32, (length, span), 0)
+    query = lax.broadcasted_iota(jnp.int32, (length, span), 1) + first
+    return jnp.where((key <= query) | (key < prefix), 0.0, NEG).astype(F32)
+
+
+def attend_kernel(group, where_ref, q_ref, k_ref, v_ref, o_ref, lse_ref, bias_ref):
+    length, span = bias_ref.shape
+
+    @pl.when(pl.program_id(0) == 0)
+    def _():
+        bias_ref[...] = mask_bias(where_ref[0], where_ref[1], length, span)
+
+    heads = q_ref.shape[1] // HD
+    pair = []
+    for h in range(heads):
+        kv = h // group
+        key = k_ref[:, HD * kv : HD * (kv + 1)]
+        value = v_ref[:, HD * kv : HD * (kv + 1)]
+        query = q_ref[:, HD * h : HD * (h + 1)] * jnp.asarray(HD**-0.5, BF)
+        scores = nt(key, query) + bias_ref[...]
+        top = jnp.max(scores, axis=0, keepdims=True)
+        exponent = jnp.exp(scores - top)
+        total = jnp.sum(exponent, axis=0, keepdims=True)
+        lse_ref[h : h + 1, :] = top + jnp.log(total)
+        mixed = tn(value, exponent.astype(BF)) / total
+        pair.append(mixed)
+        if h % 2:
+            o_ref[:, HD * (h - 1) : HD * (h + 1)] = jnp.concatenate(pair, axis=0).T.astype(BF)
+            pair = []
+
+
+def attend(where, q, kv):
+    span, length = q.shape[0], kv.shape[0]
+    blocks = kv.shape[1] // 256
+    wide = q.shape[1] // blocks
+    group = 2 * q.shape[1] // kv.shape[1]
+    return pl.pallas_call(
+        functools.partial(attend_kernel, group),
+        grid=(blocks,),
+        in_specs=[
+            pl.BlockSpec(memory_space=pltpu.SMEM),
+            pl.BlockSpec((span, wide), lambda j: (0, j)),
+            pl.BlockSpec((length, 128), lambda j: (0, j)),
+            pl.BlockSpec((length, 128), lambda j: (0, blocks + j)),
+        ],
+        out_specs=[
+            pl.BlockSpec((span, wide), lambda j: (0, j)),
+            pl.BlockSpec((wide // HD, span), lambda j: (j, 0)),
+        ],
+        out_shape=[
+            jax.ShapeDtypeStruct(q.shape, BF),
+            jax.ShapeDtypeStruct((q.shape[1] // HD, span), F32),
+        ],
+        scratch_shapes=[pltpu.VMEM((length, span), F32)],
+        compiler_params=pltpu.CompilerParams(vmem_limit_bytes=40 * 1024 * 1024),
+        cost_estimate=cost(4 * 4 * length * span * q.shape[1], 4 * span * q.shape[1], length * span * 16),
+        name="attend",
+    )(where, q, kv, kv)
+
+
+def attend_back_kernel(
+    group, where_ref, q_ref, k_ref, v_ref, do_ref, lse_ref, cos_ref, sin_ref, dq_ref, dk_ref, dv_ref, bias_ref
+):
+    length, span = bias_ref.shape
+
+    @pl.when(pl.program_id(0) == 0)
+    def _():
+        bias_ref[...] = mask_bias(where_ref[0], where_ref[1], length, span)
+
+    heads = q_ref.shape[1] // HD
+    scale = jnp.asarray(HD**-0.5, BF)
+    pair = []
+    for h in range(heads):
+        kv = h // group
+        lanes = slice(HD * kv, HD * (kv + 1))
+        key, value = k_ref[:, lanes], v_ref[:, lanes]
+        query = q_ref[:, HD * h : HD * (h + 1)] * scale
+        grad = do_ref[:, HD * h : HD * (h + 1)]
+        probs = jnp.exp(nt(key, query) + (bias_ref[...] - lse_ref[h : h + 1, :]))
+        d_probs = nt(value, grad)
+        delta = jnp.sum(probs * d_probs, axis=0, keepdims=True)
+        d_scores = (probs * (d_probs - delta)).astype(BF)
+        d_value = nn(probs.astype(BF), grad)
+        d_key = nn(d_scores, query)
+        if h % group == 0:
+            sum_key, sum_value = d_key, d_value
+        else:
+            sum_key, sum_value = sum_key + d_key, sum_value + d_value
+        if h % group == group - 1:
+            dk_ref[:, lanes] = sum_key.astype(BF)
+            dv_ref[:, lanes] = sum_value.astype(BF)
+        pair.append(tn(key * scale, d_scores))
+        if h % 2:
+            both = jnp.concatenate(pair, axis=0).T
+            back = both * cos_ref[...] - swap_halves(both) * sin_ref[...]
+            dq_ref[:, HD * (h - 1) : HD * (h + 1)] = back.astype(BF)
+            pair = []
+
+
+def attend_back(where, q, kv, d_out, lse, cosine, sine):
+    span, length = q.shape[0], kv.shape[0]
+    blocks = kv.shape[1] // 256
+    wide = q.shape[1] // blocks
+    group = 2 * q.shape[1] // kv.shape[1]
+    side = pl.BlockSpec((span, wide), lambda j: (0, j))
+    keys = pl.BlockSpec((length, 128), lambda j: (0, j))
+    table = pl.BlockSpec((span, 128), lambda j: (0, 0))
+    return pl.pallas_call(
+        functools.partial(attend_back_kernel, group),
+        grid=(blocks,),
+        in_specs=[
+            pl.BlockSpec(memory_space=pltpu.SMEM),
+            side,
+            keys,
+            pl.BlockSpec((length, 128), lambda j: (0, blocks + j)),
+            side,
+            pl.BlockSpec((wide // HD, span), lambda j: (j, 0)),
+            table,
+            table,
+        ],
+        out_specs=[side, keys, keys],
+        out_shape=[
+            jax.ShapeDtypeStruct(q.shape, BF),
+            jax.ShapeDtypeStruct((length, 128 * blocks), BF),
+            jax.ShapeDtypeStruct((length, 128 * blocks), BF),
+        ],
+        scratch_shapes=[pltpu.VMEM((length, span), F32)],
+        compiler_params=pltpu.CompilerParams(vmem_limit_bytes=40 * 1024 * 1024),
+        cost_estimate=cost(4 * 10 * length * span * q.shape[1], 8 * span * q.shape[1], length * span * 16),
+        name="attend_back",
+    )(where, q, kv, kv, d_out, lse, cosine, sine)
+
+
+def kv_back_kernel(k_ref, v_ref, cos_ref, sin_ref, dk_ref, dv_ref):
+    total = sum(k_ref[i].astype(F32) for i in range(k_ref.shape[0]))
+    for i in range(total.shape[1] // 128):
+        part = total[:, 128 * i : 128 * (i + 1)]
+        back = part * cos_ref[...] - swap_halves(part) * sin_ref[...]
+        dk_ref[:, 128 * i : 128 * (i + 1)] = back.astype(BF)
+    dv_ref[...] = sum(v_ref[i].astype(F32) for i in range(v_ref.shape[0])).astype(BF)
+
+
+def kv_back(got_key, got_value, cosine, sine):
+    return pl.pallas_call(
+        kv_back_kernel,
+        out_shape=[jax.ShapeDtypeStruct(got_key.shape[1:], BF)] * 2,
+        cost_estimate=cost(8 * got_key.size, 4 * got_key.size),
+        name="kv_back",
+    )(got_key, got_value, cosine, sine)
+
+
+def gate_parts(gate, up, d_act):
+    sig = 1.0 / (1.0 + jnp.exp(-gate))
+    silu = gate * sig
+    return (
+        (silu * up).astype(BF),
+        (d_act * up * (sig + silu * (1.0 - sig))).astype(BF),
+        (d_act * silu).astype(BF),
+    )
+
+
+def mlp_kernel(n_ref, g_ref, wg_ref, wu_ref, wd_ref, o_ref, dn_ref, o_acc, dn_acc):
+    j = pl.program_id(0)
+    normed2, grad = n_ref[...], g_ref[...]
+    gate = nn(normed2, wg_ref[...])
+    up = nn(normed2, wu_ref[...])
+    d_act = nt(grad, wd_ref[...])
+    act, d_gate, d_up = gate_parts(gate, up, d_act)
+    out = nn(act, wd_ref[...])
+    back = nt(d_gate, wg_ref[...]) + nt(d_up, wu_ref[...])
+
+    @pl.when(j == 0)
+    def _():
+        o_acc[...] = out
+        dn_acc[...] = back
+
+    @pl.when(j > 0)
+    def _():
+        o_acc[...] += out
+        dn_acc[...] += back
+
+    @pl.when(j == pl.num_programs(0) - 1)
+    def _():
+        o_ref[...] = o_acc[...].astype(BF)
+        dn_ref[...] = dn_acc[...].astype(BF)
+
+
+def mlp(normed2, grad, wg, wu, wd, step=512):
+    rows, width = normed2.shape
+    units = wg.shape[1]
+    whole = pl.BlockSpec((rows, width), lambda j: (0, 0))
+    cols = pl.BlockSpec((width, step), lambda j: (0, j))
+    return pl.pallas_call(
+        mlp_kernel,
+        grid=(units // step,),
+        in_specs=[whole, whole, cols, cols, pl.BlockSpec((step, width), lambda j: (j, 0))],
+        out_specs=[whole, whole],
+        out_shape=[jax.ShapeDtypeStruct((rows, width), BF)] * 2,
+        scratch_shapes=[pltpu.VMEM((rows, width), F32)] * 2,
+        compiler_params=pltpu.CompilerParams(vmem_limit_bytes=VMEM_MOST),
+        cost_estimate=cost(12 * rows * width * units, 6 * width * units),
+        name="mlp",
+    )(normed2, grad, wg, wu, wd)
+
+
+def unit_grads_kernel(
+    ndp, nctx, pieces, chunk, rows, *refs
+):
+    n_in = refs[:pieces]
+    g_in = refs[pieces : 2 * pieces]
+    wg_hbm, wu_hbm, wd_hbm = refs[2 * pieces : 2 * pieces + 3]
+    outs = refs[2 * pieces + 3 : 2 * pieces + 9]
+    (
+        n_all, g_all, wg_buf, wu_buf, wd_buf, act, d_gate, d_up,
+        give, take, in_sem, w_sem, send_sem, recv_sem,
+    ) = refs[2 * pieces + 9 :]
+    tokens, width = n_all.shape
+    units = act.shape[1]
+    me = lax.axis_index("ctx")
+    core = me % 2
+    xpos = me // 2
+    nx = nctx // 2
+    start = lax.axis_index("dp") * units
+    mate = {"ctx": me + 1 - 2 * core}
+
+    barrier = pltpu.get_barrier_semaphore()
+    pl.semaphore_signal(barrier, inc=1, device_id=mate, device_id_type=pl.DeviceIdType.MESH)
+
+    loads = []
+    for which, (srcs, dst) in enumerate(((n_in, n_all), (g_in, g_all))):
+        at = 0
+        for i, src in enumerate(srcs):
+            n = src.shape[0]
+            loads.append(
+                pltpu.make_async_copy(src, dst.at[pl.ds(at, n)], in_sem.at[which * pieces + i])
+            )
+            at += n
+
+    def weights(j, slot):
+        at = pl.multiple_of(start + j * chunk, chunk)
+        return (
+            pltpu.make_async_copy(wg_hbm.at[:, pl.ds(at, chunk)], wg_buf.at[slot], w_sem.at[slot, 0]),
+            pltpu.make_async_copy(wu_hbm.at[:, pl.ds(at, chunk)], wu_buf.at[slot], w_sem.at[slot, 1]),
+            pltpu.make_async_copy(wd_hbm.at[pl.ds(at, chunk)], wd_buf.at[slot], w_sem.at[slot, 2]),
+        )
+
+    for copy in weights(0, 0):
+        copy.start()
+    for copy in loads:
+        copy.start()
+    for copy in loads:
+        copy.wait()
+
+    count = units // chunk
+
+    @pl.loop(0, count)
+    def _(j):
+        slot = j % 2
+        for copy in weights(j, slot):
+            copy.wait()
+
+        @pl.when(j + 1 < count)
+        def _():
+            for copy in weights(j + 1, 1 - slot):
+                copy.start()
+
+        cols = pl.ds(pl.multiple_of(j * chunk, chunk), chunk)
+
+        @pl.loop(0, tokens // rows)
+        def _(i):
+            some = pl.ds(pl.multiple_of(i * rows, rows), rows)
+            gate = nn(n_all[some], wg_buf[slot])
+            up = nn(n_all[some], wu_buf[slot])
+            d_act = nt(g_all[some], wd_buf[slot])
+            a, dg, du = gate_parts(gate, up, d_act)
+            act[some, cols] = a
+            d_gate[some, cols] = dg
+            d_up[some, cols] = du
+
+    pl.semaphore_wait(barrier, 1)
+
+    part = width // (ndp * nctx)
+    terms = ((g_all, act), (n_all, d_gate), (n_all, d_up))
+
+    def product(w, x, c):
+        left, right = terms[w]
+        block = jnp.concatenate(
+            [
+                left[:, pl.ds(pl.multiple_of((z * nctx + x * 2 + c) * part, part), part)]
+                for z in range(ndp)
+            ],
+            axis=1,
+        )
+        return tn(block, right[...])
+
+    copies = [
+        pltpu.make_async_remote_copy(
+            src_ref=give.at[w],
+            dst_ref=take.at[w],
+            send_sem=send_sem.at[w],
+            recv_sem=recv_sem.at[w],
+            device_id=mate,
+            device_id_type=pl.DeviceIdType.MESH,
+        )
+        for w in range(3)
+    ]
+
+    def hand(w):
+        for i in range(nx):
+            x = (xpos + 1 + i) % nx
+            give[w, i] = product(w, x, 1 - core).astype(BF)
+        copies[w].start()
+
+    def keep(w):
+        parts = [product(w, (xpos + 1 + i) % nx, core) for i in range(nx)]
+        copies[w].wait()
+        for i in range(nx):
+            outs[2 * w + i][...] = (parts[i] + take[w, i].astype(F32)).astype(BF)
+
+    hand(0)
+    hand(1)
+    keep(0)
+    hand(2)
+    keep(1)
+    keep(2)
+
+
+def unit_grads(n_pieces, g_pieces, wg, wu, wd, ndp, nctx, chunk=256, rows=512):
+    pieces = len(n_pieces)
+    tokens = sum(p.shape[0] for p in n_pieces)
+    width = wg.shape[0]
+    units = wg.shape[1] // ndp
+    part = width // (ndp * nctx)
+    nx = nctx // 2
+    hbm = pl.BlockSpec(memory_space=pl.ANY)
+    vmem = pl.BlockSpec(memory_space=pltpu.VMEM)
+    return pl.pallas_call(
+        functools.partial(unit_grads_kernel, ndp, nctx, pieces, chunk, rows),
+        in_specs=[hbm] * (2 * pieces + 3),
+        out_specs=[vmem] * 6,
+        out_shape=[jax.ShapeDtypeStruct((ndp * part, units), BF)] * 6,
+        scratch_shapes=[
+            pltpu.VMEM((tokens, width), BF),
+            pltpu.VMEM((tokens, width), BF),
+            pltpu.VMEM((2, width, chunk), BF),
+            pltpu.VMEM((2, width, chunk), BF),
+            pltpu.VMEM((2, chunk, width), BF),
+            pltpu.VMEM((tokens, units), BF),
+            pltpu.VMEM((tokens, units), BF),
+            pltpu.VMEM((tokens, units), BF),
+            pltpu.VMEM((3, nx, ndp * part, units), BF),
+            pltpu.VMEM((3, nx, ndp * part, units), BF),
+            pltpu.SemaphoreType.DMA((2 * pieces,)),
+            pltpu.SemaphoreType.DMA((2, 3)),
+            pltpu.SemaphoreType.DMA((3,)),
+            pltpu.SemaphoreType.DMA((3,)),
+        ],
+        compiler_params=pltpu.CompilerParams(
+            vmem_limit_bytes=VMEM_MOST, collective_id=0, has_side_effects=True
+        ),
+        cost_estimate=cost(12 * tokens * width * units, 2 * (2 * tokens + 3 * units) * width),
+        name="unit_grads",
+    )(*n_pieces, *g_pieces, wg, wu, wd)
 
 
 def dot_plain(left, right):
@@ -279,10 +742,157 @@
     return local
 
 
+def suits(ndp, nctx, nten, layer_input, output_grad, prefix, attn_gain, w_query, w_key, w_value, w_out, mlp_gain, w_gate, w_up, w_down):
+    seqs, span, width = layer_input.shape
+    return (
+        seqs == 1
+        and nctx == 4
+        and nten == 2
+        and ndp > 1
+        and span % 256 == 0
+        and width % (128 * ndp * nctx) == 0
+        and w_key.shape[1] % 128 == 0
+        and w_query.shape[1] % 256 == 0
+        and w_gate.shape[1] % (512 * ndp) == 0
+    )
+
+
+def build_fast(ndp, nctx, nten):
+    def pull(v, axis, n, s):
+        return lax.ppermute(v, axis, [((i + s) % n, i) for i in range(n)])
+
+    def flip(v, axis, n, bit):
+        return lax.ppermute(v, axis, [(i, i ^ bit) for i in range(n)])
+
+    def gather_dp(v):
+        half = v.shape[0] // 2
+        part = lax.dynamic_slice_in_dim(v, lax.axis_index("tensor") * half, half, 0)
+        pieces = [v]
+        for s in range(1, ndp):
+            got = pull(part, "dp", ndp, s)
+            pieces += [got, flip(got, "tensor", 2, 1)]
+        return pieces
+
+    def ctx_sum(full):
+        r = full.shape[0] // (ndp * nctx)
+        me = lax.axis_index("ctx")
+        work = full.reshape(ndp, nctx, r, full.shape[1])
+        bit = 1
+        while bit < nctx:
+            left = work.shape[1] // 2
+            work = work.reshape(ndp, left, 2, r, full.shape[1])
+            mine = (me // bit) % 2
+            keep = lax.dynamic_index_in_dim(work, mine, 2, keepdims=False)
+            give = lax.dynamic_index_in_dim(work, 1 - mine, 2, keepdims=False)
+            got = flip(give, "ctx", nctx, bit)
+            work = (keep.astype(F32) + got.astype(F32)).astype(BF)
+            bit *= 2
+        return work.reshape(ndp, r, full.shape[1])
+
+    def finish_sum(full):
+        got = lax.all_to_all(ctx_sum(full), "dp", 0, 0, tiled=True)
+        return jnp.sum(got.astype(F32), axis=0)
+
+    def local(
+        layer_input,
+        output_grad,
+        prefix,
+        attn_gain,
+        w_query,
+        w_key,
+        w_value,
+        w_out,
+        mlp_gain,
+        w_gate,
+        w_up,
+        w_down,
+    ):
+        seqs, span, width = layer_input.shape
+        kvw = w_key.shape[1]
+        low = layer_input.reshape(span, width)
+        rows = low.astype(F32)
+        grad_low = output_grad.reshape(span, width)
+        grad_pieces = gather_dp(grad_low)
+        first = lax.axis_index("ctx") * span
+        where = jnp.stack([first, prefix[0]]).astype(jnp.int32)
+        cosine, sine = rope_tables(first, span)
+        normed1, query, kv = qkv(low, attn_gain, w_query, w_key, w_value, cosine, sine)
+        kv_all = lax.all_gather(kv, "ctx", axis=0, tiled=True)
+        attended, lse = attend(where, query, kv_all)
+        part = dot_plain(attended, w_out).astype(BF)
+        resid = rows + (part.astype(F32) + flip(part, "tensor", 2, 1).astype(F32))
+        normed2 = normed(resid, mlp_gain).astype(BF)
+        normed2_pieces = gather_dp(normed2)
+
+        out_part, back_part = mlp(normed2, grad_low, w_gate, w_up, w_down)
+        back = back_part.astype(F32) + flip(back_part, "tensor", 2, 1).astype(F32)
+        output = resid + (out_part.astype(F32) + flip(out_part, "tensor", 2, 1).astype(F32))
+        output = output.astype(BF).reshape(seqs, span, width)
+
+        pairs = unit_grads(normed2_pieces, grad_pieces, w_gate, w_up, w_down, ndp, nctx)
+        grads = []
+        for w in range(3):
+            give, keep = pairs[2 * w : 2 * w + 2]
+            got = flip(give, "ctx", nctx, 2)
+            total = (keep.astype(F32) + got.astype(F32)).astype(BF)
+            total = total.reshape(ndp, -1, total.shape[1])
+            grads.append(lax.all_to_all(total, "dp", 0, 0, tiled=True))
+        s_down = jnp.swapaxes(grads[0], 1, 2).reshape(w_down.shape[0], -1).astype(F32)
+        s_gate, s_up = (
+            jnp.swapaxes(g, 0, 1).reshape(g.shape[1], -1).astype(F32) for g in grads[1:]
+        )
+
+        d_resid_norm, g_mlp_gain = norm_back(resid, mlp_gain, back)
+        d_resid = grad_low.astype(F32) + d_resid_norm
+        d_resid_low = d_resid.astype(BF)
+        d_attended = dot_right(d_resid_low, w_out).astype(BF)
+        s_out = finish_sum(dot_left(d_resid_low, attended).astype(BF)).T
+        d_qp, d_key, d_value = attend_back(
+            where, query, kv_all, d_attended, lse, cosine, sine
+        )
+        got_key = lax.all_to_all(d_key.reshape(nctx, span, kvw), "ctx", 0, 0, tiled=True)
+        got_value = lax.all_to_all(d_value.reshape(nctx, span, kvw), "ctx", 0, 0, tiled=True)
+        d_kp, d_vp = kv_back(got_key, got_value, cosine, sine)
+        front = dot_right(d_qp, w_query) + dot_right(d_kp, w_key) + dot_right(d_vp, w_value)
+        front = front.astype(BF)
+        d_normed1 = front.astype(F32) + flip(front, "tensor", 2, 1).astype(F32)
+        d_rows_norm, g_attn_gain = norm_back(rows, attn_gain, d_normed1)
+        d_input = (d_resid + d_rows_norm).reshape(seqs, span, width)
+        s_qkv = finish_sum(
+            dot_left(normed1, jnp.concatenate([d_qp, d_kp, d_vp], axis=1)).astype(BF)
+        )
+        nq = w_query.shape[1]
+        s_query, s_key, s_value = s_qkv[:, :nq], s_qkv[:, nq : nq + kvw], s_qkv[:, nq + kvw :]
+        gains = jnp.stack([g_attn_gain, g_mlp_gain])
+        gains = jnp.swapaxes(gains.reshape(2, ndp * nctx, -1), 0, 1)
+        gains = lax.all_to_all(gains, ("dp", "ctx"), 0, 0, tiled=True)
+        gains = jnp.sum(gains, axis=0)
+        return (
+            output,
+            d_input,
+            gains[0],
+            s_query,
+            s_key,
+            s_value,
+            s_out,
+            gains[1],
+            s_gate,
+            s_up,
+            s_down,
+        )
+
+    return local
+
+
 def solution(mesh):
-    sizes = mesh.shape
+    sizes = mesh.shape["dp"], mesh.shape["ctx"], mesh.shape["tensor"]
+    plain, fast = build(*sizes), build_fast(*sizes)
+
+    def local(*args):
+        return (fast if suits(*sizes, *args) else plain)(*args)
+
     return jax.shard_map(
-        build(sizes["dp"], sizes["ctx"], sizes["tensor"]),
+        local,
         mesh=mesh,
         in_specs=(
             P("dp", "ctx", None),

time: 585 us -> 559 us (0.956)
  the two profiles are of different devices: /device:TPU:25 before, /device:TPU:0 now
where the time goes in v2:
time: 559 us; the launch traced here: 551 us
  waiting for transfers between devices  258 us (46%)
  Pallas kernels  111 us (20%)
  starting transfers between devices  70.7 us (13%)
  other arithmetic  45 us (8%)
  local copies, waits for them, and re-layouts  34.8 us (6%)
  matrix products  16.1 us (3%)
  between operations  15.4 us (3%)
    ppermute x17, waiting for transfers between devices, flip(): return lax.ppermute(v, axis, [(i, i ^ bit) for i in range(n)])  134 us
    pallas_call x1, Pallas kernels, unit_grads(): pl.pallas_call(functools.partial(unit_grads_kernel, ndp, nctx, pieces, ch...  38 us
    pallas_call x1, Pallas kernels, mlp(): pl.pallas_call(mlp_kernel, grid=(units // step,), in_specs=[whole, whole,...  37.6 us
    ppermute x6, waiting for transfers between devices, pull(): return lax.ppermute(v, axis, [((i + s) % n, i) for i in range(n)])  33.3 us
    all_to_all x3, waiting for transfers between devices, local(): grads.append(lax.all_to_all(total, 'dp', 0, 0, tiled=True))  28.3 us
    all_to_all x2, waiting for transfers between devices, finish_sum(): got = lax.all_to_all(ctx_sum(full), 'dp', 0, 0, tiled=True)  20.4 us
    all_to_all x1, waiting for transfers between devices, local(): gains = lax.all_to_all(gains, ('dp', 'ctx'), 0, 0, tiled=True)  19.1 us
    all_gather x1, waiting for transfers between devices, local(): kv_all = lax.all_gather(kv, 'ctx', axis=0, tiled=True)  18.9 us
  transfers between devices with their start and end apart: 32, of which 17 were waited for; matrix products, arithmetic and copies ran while one was open for 14% of the time, Pallas kernels for 10%

profile of v2, /device:TPU:0, one launch (start us, length us, event | category | flops | bytes accessed | tf_op | source)
XLA Modules:
  0.0 550.9 jit_solution(17524440514974953601)
XLA Ops:
  14.8 4.8 qkv.1
  20.3 18.9 %all-gather.2.cloned.1.call-done.k_ref.v_ref = bf16[1024,512]{1,0:T(8,128)(2,1)} async-done(((bf16[256,512]{1,0:T(8,128)(2,1)}), bf16[1024,512]{1,0:T(8,128)(2,1)}) %all-gather.2.cloned.1.call-update) | async-done | bytes 1048592 | tf_op jit(solution)/shard_map/all_gather | solution.py:820
  40.4 12.2 %attend.1 = (bf16[256,1024]{1,0:T(8,128)(2,1)S(1)}, f32[16,256]{1,0:T(8,128)S(1)}) custom-call(s32[2]{0:T(128)S(1)} %pad_add_fusion.where_ref, bf16[256,1024]{1,0:T(8,128)(2,1)S(1)} %get-tuple-element.29.q_ref, bf16[1024,512]{1,0:T(8,128)(2,1)S(1)} %copy-done.15, bf16[1024,512]{1,0:T(8,128)(2,1)S(1)} %copy-done.15), custom_call_target="tpu_custom_call" | custom-call | flops 4294967296 | bytes 1048576 | tf_op jit(solution)/shard_map/attend/pallas_call | solution.py:150
  55.4 23.8 %collective-permute-done = bf16[256,2048]{1,0:T(8,128)(2,1)S(1)} collective-permute-done((bf16[256,2048]{1,0:T(8,128)(2,1)S(1)}, bf16[256,2048]{1,0:T(8,128)(2,1)S(1)}, u32[]{:S(2)}, u32[]{:S(2)}) %collective-permute-start) | collective-permute-done | bytes 1048608 | tf_op jit(solution)/shard_map/ppermute | solution.py:765
  82.5 37.6 %mlp.1 = (bf16[256,2048]{1,0:T(8,128)(2,1)}, bf16[256,2048]{1,0:T(8,128)(2,1)}) custom-call(bf16[256,2048]{1,0:T(8,128)(2,1)} %multiply_convert_fusion.n_ref.refs_0_, bf16[256,2048]{1,0:T(8,128)(2,1)} %bitcast.80, bf16[2048,4096]{1,0:T(8,128)(2,1)} %refs_14_.1, bf16[2048,4096]{1,0:T(8,128)(2,1)} %refs_15_.1, bf16[4096,2048]{1,0:T(8,128)(2,1)} %refs_16_.1), custom_call_target="tpu_custom_call" | custom-call | flops 25769803776 | bytes 50331648 | tf_op jit(solution)/shard_map/mlp/pallas_call | solution.py:306
  127.5 19.0 %collective-permute-done.2 = bf16[256,2048]{1,0:T(8,128)(2,1)} collective-permute-done((bf16[256,2048]{1,0:T(8,128)(2,1)}, bf16[256,2048]{1,0:T(8,128)(2,1)}, u32[]{:S(2)}, u32[]{:S(2)}) %collective-permute-start.2) | collective-permute-done | bytes 1048608 | tf_op jit(solution)/shard_map/ppermute | solution.py:765
  149.5 17.8 %collective-permute-done.1 = bf16[256,2048]{1,0:T(8,128)(2,1)} collective-permute-done((bf16[256,2048]{1,0:T(8,128)(2,1)}, bf16[256,2048]{1,0:T(8,128)(2,1)}, u32[]{:S(2)}, u32[]{:S(2)}) %collective-permute-start.1) | collective-permute-done | bytes 1048608 | tf_op jit(solution)/shard_map/ppermute | solution.py:765
  167.4 3.9 multiply_add_fusion
  173.3 16.1 %attend_back.1 = (bf16[256,1024]{1,0:T(8,128)(2,1)S(1)}, bf16[1024,256]{1,0:T(8,128)(2,1)}, bf16[1024,256]{1,0:T(8,128)(2,1)}) custom-call(s32[2]{0:T(128)S(1)} %pad_add_fusion.where_ref, bf16[256,1024]{1,0:T(8,128)(2,1)S(1)} %get-tuple-element.29.q_ref, bf16[1024,512]{1,0:T(8,128)(2,1)S(1)} %copy-done.16, bf16[1024,512]{1,0:T(8,128)(2,1)S(1)} %copy-done.16, ...), custom_call_target="tpu_custom_call" | custom-call | flops 10737418240 | bytes 2097152 | tf_op jit(solution)/shard_map/attend_back/pallas_call | solution.py:221
  203.0 4.1 all-to-all-start.1
  207.2 5.0 fusion.28
  222.8 32.2 %collective-permute-done.10.refs_3_ = bf16[128,2048]{1,0:T(8,128)(2,1)} collective-permute-done((bf16[128,2048]{1,0:T(8,128)(2,1)}, bf16[128,2048]{1,0:T(8,128)(2,1)}, u32[]{:S(2)}, u32[]{:S(2)}) %collective-permute-start.10) | collective-permute-done | bytes 524320 | tf_op jit(solution)/shard_map/ppermute | solution.py:762
  261.3 8.8 %collective-permute-done.11.refs_4_ = bf16[128,2048]{1,0:T(8,128)(2,1)} collective-permute-done((bf16[128,2048]{1,0:T(8,128)(2,1)}, bf16[128,2048]{1,0:T(8,128)(2,1)}, u32[]{:S(2)}, u32[]{:S(2)}) %collective-permute-start.11) | collective-permute-done | bytes 524320 | tf_op jit(solution)/shard_map/ppermute | solution.py:765
  270.1 11.2 %collective-permute-done.13.refs_6_ = bf16[128,2048]{1,0:T(8,128)(2,1)} collective-permute-done((bf16[128,2048]{1,0:T(8,128)(2,1)}, bf16[128,2048]{1,0:T(8,128)(2,1)}, u32[]{:S(2)}, u32[]{:S(2)}) %collective-permute-start.13) | collective-permute-done | bytes 524320 | tf_op jit(solution)/shard_map/ppermute | solution.py:765
  281.3 38.0 %unit_grads.1 = (bf16[512,1024]{1,0:T(8,128)(2,1)}, bf16[512,1024]{1,0:T(8,128)(2,1)}, bf16[512,1024]{1,0:T(8,128)(2,1)}, bf16[512,1024]{1,0:T(8,128)(2,1)}, bf1...) custom-call(bf16[256,2048]{1,0:T(8,128)(2,1)} %multiply_convert_fusion.n_ref.refs_0_, ...), custom_call_target="tpu_custom_call" | custom-call | flops 25769803776 | bytes 20971520 | tf_op jit(solution)/shard_map/unit_grads/pallas_call | solution.py:450
  321.4 4.5 convolution_convert_fusion
  328.7 9.1 %all-to-all-start.2 = ((f32[16,2,128]{2,1,0:T(2,128)}), f32[16,2,128]{2,1,0:T(2,128)S(1)}, u32[]{:S(2)}, u32[]{:S(2)}) async-start(f32[16,2,128]{2,1,0:T(2,128)} %maximum_bitcast_fusion), calls=%async_computation.2 | async-start | bytes 32768 | tf_op jit(solution)/shard_map/all_to_all | solution.py:868
  337.9 7.9 %collective-permute-done.20 = bf16[512,1024]{1,0:T(8,128)(2,1)} collective-permute-done((bf16[512,1024]{1,0:T(8,128)(2,1)}, bf16[512,1024]{1,0:T(8,128)(2,1)}, u32[]{:S(2)}, u32[]{:S(2)}) %collective-permute-start.20) | collective-permute-done | bytes 1048608 | tf_op jit(solution)/shard_map/ppermute | solution.py:765
  348.4 19.1 %all-to-all-done.2 = f32[16,2,128]{2,1,0:T(2,128)S(1)} async-done(((f32[16,2,128]{2,1,0:T(2,128)}), f32[16,2,128]{2,1,0:T(2,128)S(1)}, u32[]{:S(2)}, u32[]{:S(2)}) %all-to-all-start.2) | async-done | bytes 16416 | tf_op jit(solution)/shard_map/all_to_all | solution.py:868
  367.5 9.0 %all-to-all-start.5 = ((bf16[4,128,1024]{2,1,0:T(8,128)(2,1)}), bf16[4,128,1024]{2,1,0:T(8,128)(2,1)S(1)}, u32[]{:S(2)}, u32[]{:S(2)}) async-start(bf16[4,128,1024]{2,1,0:T(8,128)(2,1)} %bitcast.79), calls=%async_computation.5 | async-start | bytes 2097152 | tf_op jit(solution)/shard_map/all_to_all | solution.py:839
  376.6 4.0 dynamic-slice_bitcast_fusion
  388.6 14.0 %all-to-all-done.5 = bf16[4,128,1024]{2,1,0:T(8,128)(2,1)S(1)} async-done(((bf16[4,128,1024]{2,1,0:T(8,128)(2,1)}), bf16[4,128,1024]{2,1,0:T(8,128)(2,1)S(1)}, u32[]{:S(2)}, u32[]{:S(2)}) %all-to-all-start.5) | async-done | bytes 1048608 | tf_op jit(solution)/shard_map/all_to_all | solution.py:839
  402.6 4.3 all-to-all-start.6
  406.9 4.2 collective-permute-done.22
  417.9 14.3 %all-to-all-done.6 = bf16[4,128,1024]{2,1,0:T(8,128)(2,1)} async-done(((bf16[4,128,1024]{2,1,0:T(8,128)(2,1)}), bf16[4,128,1024]{2,1,0:T(8,128)(2,1)}, u32[]{:S(2)}, u32[]{:S(2)}) %all-to-all-start.6) | async-done | bytes 1048608 | tf_op jit(solution)/shard_map/all_to_all | solution.py:839
  432.2 4.2 all-to-all-start.7
  447.3 17.7 %collective-permute-done.7 = bf16[4,1,128,1024]{3,2,0,1:T(8,128)(2,1)} collective-permute-done((bf16[4,1,128,1024]{3,2,0,1:T(8,128)(2,1)}, bf16[4,1,128,1024]{3,2,0,1:T(8,128)(2,1)}, u32[]{:S(2)}, u32[]{:S(2)}) %collective-permute-start.7) | collective-permute-done | bytes 1048608 | tf_op jit(solution)/shard_map/ppermute | solution.py:765
  468.0 5.0 all-to-all-start.4
  473.0 23.9 %collective-permute-done.5 = bf16[4,1,128,1536]{3,2,1,0:T(8,128)(2,1)} collective-permute-done((bf16[4,1,128,1536]{3,2,1,0:T(8,128)(2,1)}, bf16[4,1,128,1536]{3,2,1,0:T(8,128)(2,1)}, u32[]{:S(2)}, u32[]{:S(2)}) %collective-permute-start.5) | collective-permute-done | bytes 1572896 | tf_op jit(solution)/shard_map/ppermute | solution.py:765
  500.4 4.9 all-to-all-start.3
  505.3 3.9 fusion.10
  520.2 20.4 %all-to-all-done.3 = bf16[4,128,1536]{2,1,0:T(8,128)(2,1)} async-done(((bf16[4,128,1536]{2,1,0:T(8,128)(2,1)}), bf16[4,128,1536]{2,1,0:T(8,128)(2,1)}, u32[]{:S(2)}, u32[]{:S(2)}) %all-to-all-start.3) | async-done | bytes 1572896 | tf_op jit(solution)/shard_map/all_to_all | solution.py:793
  (157 shorter events, 111.4 us)
Async XLA Ops:
  7.2 32.0 %all-gather.2.cloned.1.call-start = ((), (), s32[]{:S(2)}) async-start(), calls=%async_computation.8 | async-start | bytes 1310720 | tf_op jit(solution)/shard_map/all_gather | solution.py:820
  53.9 25.4 %collective-permute-start = (bf16[256,2048]{1,0:T(8,128)(2,1)S(1)}, bf16[256,2048]{1,0:T(8,128)(2,1)S(1)}, u32[]{:S(2)}, u32[]{:S(2)}) collective-permute-start(bf16[256,2048]{1,0:T(8,128)(2,1)S(1)} %convolution_convert_fusion.2), channel_id=1, source_target_pairs={{0,1},{1,0},{2,3},{3,2},{4,5},{5,4},{6,7},{7,6},{8,9},{9,8},{10,11... | collective-permute-start | bytes 3145736 | tf_op jit(solution)/shard_map/ppermute | solution.py:765
  120.1 26.3 %collective-permute-start.2 = (bf16[256,2048]{1,0:T(8,128)(2,1)}, bf16[256,2048]{1,0:T(8,128)(2,1)}, u32[]{:S(2)}, u32[]{:S(2)}) collective-permute-start(bf16[256,2048]{1,0:T(8,128)(2,1)} %get-tuple-element.33), channel_id=1, source_target_pairs={{0,1},{1,0},{2,3},{3,2},{4,5},{5,4},{6,7},{7,6},{8,9},{9,8},{10,11... | collective-permute-start | bytes 3145736 | tf_op jit(solution)/shard_map/ppermute | solution.py:765
  121.6 45.7 %collective-permute-start.1 = (bf16[256,2048]{1,0:T(8,128)(2,1)}, bf16[256,2048]{1,0:T(8,128)(2,1)}, u32[]{:S(2)}, u32[]{:S(2)}) collective-permute-start(bf16[256,2048]{1,0:T(8,128)(2,1)} %get-tuple-element.32), channel_id=1, source_target_pairs={{0,1},{1,0},{2,3},{3,2},{4,5},{5,4},{6,7},{7,6},{8,9},{9,8},{10,11... | collective-permute-start | bytes 3145736 | tf_op jit(solution)/shard_map/ppermute | solution.py:765
  124.1 71.0 %collective-permute-start.14 = (bf16[128,2048]{1,0:T(8,128)(2,1)}, bf16[128,2048]{1,0:T(8,128)(2,1)}, u32[]{:S(2)}, u32[]{:S(2)}) collective-permute-start(bf16[128,2048]{1,0:T(8,128)(2,1)} %dynamic-slice_bitcast_fusion.1), channel_id=1, source_target_pairs={{8,0},{16,8},{24,16},{0,24},{9,1},{17,9},{25,17},{1,25},{10,2},{18... | collective-permute-start | bytes 1572872 | tf_op jit(solution)/shard_map/ppermute | solution.py:762
  127.5 74.0 %collective-permute-start.16 = (bf16[128,2048]{1,0:T(8,128)(2,1)}, bf16[128,2048]{1,0:T(8,128)(2,1)}, u32[]{:S(2)}, u32[]{:S(2)}) collective-permute-start(bf16[128,2048]{1,0:T(8,128)(2,1)} %dynamic-slice_bitcast_fusion.1), channel_id=1, source_target_pairs={{16,0},{24,8},{0,16},{8,24},{17,1},{25,9},{1,17},{9,25},{18,2},{26... | collective-permute-start | bytes 1572872 | tf_op jit(solution)/shard_map/ppermute | solution.py:762
  190.1 12.8 %all-to-all-start = ((bf16[4,256,256]{2,1,0:T(8,128)(2,1)}), bf16[4,256,256]{2,1,0:T(8,128)(2,1)S(1)}, u32[]{:S(2)}, u32[]{:S(2)}) async-start(bf16[4,256,256]{2,1,0:T(8,128)(2,1)} %bitcast.5), calls=%async_computation | async-start | bytes 1048576 | tf_op jit(solution)/shard_map/all_to_all | solution.py:853
  193.6 24.6 %collective-permute-start.18 = (bf16[128,2048]{1,0:T(8,128)(2,1)}, bf16[128,2048]{1,0:T(8,128)(2,1)}, u32[]{:S(2)}, u32[]{:S(2)}) collective-permute-start(bf16[128,2048]{1,0:T(8,128)(2,1)} %dynamic-slice_bitcast_fusion.1), channel_id=1, source_target_pairs={{24,0},{0,8},{8,16},{16,24},{25,1},{1,9},{9,17},{17,25},{26,2},{2,... | collective-permute-start | bytes 1572872 | tf_op jit(solution)/shard_map/ppermute | solution.py:762
  195.2 23.9 %collective-permute-start.15 = (bf16[128,2048]{1,0:T(8,128)(2,1)}, bf16[128,2048]{1,0:T(8,128)(2,1)}, u32[]{:S(2)}, u32[]{:S(2)}) collective-permute-start(bf16[128,2048]{1,0:T(8,128)(2,1)} %collective-permute-done.14.refs_8_), channel_id=1, source_target_pairs={{0,1},{1,0},{2,3},{3,2},{4,5},{5,4},{6,7},{7,6},{8,9},{9,8},{10,11... | collective-permute-start | bytes 1572872 | tf_op jit(solution)/shard_map/ppermute | solution.py:765
  198.5 22.7 %collective-permute-start.8 = (bf16[128,2048]{1,0:T(8,128)(2,1)}, bf16[128,2048]{1,0:T(8,128)(2,1)}, u32[]{:S(2)}, u32[]{:S(2)}) collective-permute-start(bf16[128,2048]{1,0:T(8,128)(2,1)} %constant_dynamic-slice_fusion), channel_id=1, source_target_pairs={{8,0},{16,8},{24,16},{0,24},{9,1},{17,9},{25,17},{1,25},{10,2},{18... | collective-permute-start | bytes 1572872 | tf_op jit(solution)/shard_map/ppermute | solution.py:762
  200.9 54.1 %collective-permute-start.10 = (bf16[128,2048]{1,0:T(8,128)(2,1)}, bf16[128,2048]{1,0:T(8,128)(2,1)}, u32[]{:S(2)}, u32[]{:S(2)}) collective-permute-start(bf16[128,2048]{1,0:T(8,128)(2,1)} %constant_dynamic-slice_fusion), channel_id=1, source_target_pairs={{16,0},{24,8},{0,16},{8,24},{17,1},{25,9},{1,17},{9,25},{18,2},{26... | collective-permute-start | bytes 1572872 | tf_op jit(solution)/shard_map/ppermute | solution.py:762
  201.5 55.0 %collective-permute-start.12 = (bf16[128,2048]{1,0:T(8,128)(2,1)}, bf16[128,2048]{1,0:T(8,128)(2,1)}, u32[]{:S(2)}, u32[]{:S(2)}) collective-permute-start(bf16[128,2048]{1,0:T(8,128)(2,1)} %constant_dynamic-slice_fusion), channel_id=1, source_target_pairs={{24,0},{0,8},{8,16},{16,24},{25,1},{1,9},{9,17},{17,25},{26,2},{2,... | collective-permute-start | bytes 1572872 | tf_op jit(solution)/shard_map/ppermute | solution.py:762
  203.0 13.0 %all-to-all-start.1 = ((bf16[4,256,256]{2,1,0:T(8,128)(2,1)}), bf16[4,256,256]{2,1,0:T(8,128)(2,1)}, u32[]{:S(2)}, u32[]{:S(2)}) async-start(bf16[4,256,256]{2,1,0:T(8,128)(2,1)} %bitcast.6), calls=%async_computation.1 | async-start | bytes 1048576 | tf_op jit(solution)/shard_map/all_to_all | solution.py:854
  218.2 41.6 %collective-permute-start.17 = (bf16[128,2048]{1,0:T(8,128)(2,1)}, bf16[128,2048]{1,0:T(8,128)(2,1)}, u32[]{:S(2)}, u32[]{:S(2)}) collective-permute-start(bf16[128,2048]{1,0:T(8,128)(2,1)} %collective-permute-done.16.refs_10_), channel_id=1, source_target_pairs={{0,1},{1,0},{2,3},{3,2},{4,5},{5,4},{6,7},{7,6},{8,9},{9,8},{10,11... | collective-permute-start | bytes 1572872 | tf_op jit(solution)/shard_map/ppermute | solution.py:765
  219.1 42.2 %collective-permute-start.19 = (bf16[128,2048]{1,0:T(8,128)(2,1)}, bf16[128,2048]{1,0:T(8,128)(2,1)}, u32[]{:S(2)}, u32[]{:S(2)}) collective-permute-start(bf16[128,2048]{1,0:T(8,128)(2,1)} %collective-permute-done.18.refs_12_), channel_id=1, source_target_pairs={{0,1},{1,0},{2,3},{3,2},{4,5},{5,4},{6,7},{7,6},{8,9},{9,8},{10,11... | collective-permute-start | bytes 1572872 | tf_op jit(solution)/shard_map/ppermute | solution.py:765
  221.3 40.1 %collective-permute-start.9 = (bf16[128,2048]{1,0:T(8,128)(2,1)}, bf16[128,2048]{1,0:T(8,128)(2,1)}, u32[]{:S(2)}, u32[]{:S(2)}) collective-permute-start(bf16[128,2048]{1,0:T(8,128)(2,1)} %collective-permute-done.8.refs_1_), channel_id=1, source_target_pairs={{0,1},{1,0},{2,3},{3,2},{4,5},{5,4},{6,7},{7,6},{8,9},{9,8},{10,11... | collective-permute-start | bytes 1572872 | tf_op jit(solution)/shard_map/ppermute | solution.py:765
  255.0 15.1 %collective-permute-start.11 = (bf16[128,2048]{1,0:T(8,128)(2,1)}, bf16[128,2048]{1,0:T(8,128)(2,1)}, u32[]{:S(2)}, u32[]{:S(2)}) collective-permute-start(bf16[128,2048]{1,0:T(8,128)(2,1)} %collective-permute-done.10.refs_3_), channel_id=1, source_target_pairs={{0,1},{1,0},{2,3},{3,2},{4,5},{5,4},{6,7},{7,6},{8,9},{9,8},{10,11... | collective-permute-start | bytes 1572872 | tf_op jit(solution)/shard_map/ppermute | solution.py:765
  256.5 24.9 %collective-permute-start.13 = (bf16[128,2048]{1,0:T(8,128)(2,1)}, bf16[128,2048]{1,0:T(8,128)(2,1)}, u32[]{:S(2)}, u32[]{:S(2)}) collective-permute-start(bf16[128,2048]{1,0:T(8,128)(2,1)} %collective-permute-done.12.refs_5_), channel_id=1, source_target_pairs={{0,1},{1,0},{2,3},{3,2},{4,5},{5,4},{6,7},{7,6},{8,9},{9,8},{10,11... | collective-permute-start | bytes 1572872 | tf_op jit(solution)/shard_map/ppermute | solution.py:765
  259.8 66.1 %collective-permute-start.3 = (bf16[256,2048]{1,0:T(8,128)(2,1)S(1)}, bf16[256,2048]{1,0:T(8,128)(2,1)}, u32[]{:S(2)}, u32[]{:S(2)}) collective-permute-start(bf16[256,2048]{1,0:T(8,128)(2,1)S(1)} %fusion.5), channel_id=1, source_target_pairs={{0,1},{1,0},{2,3},{3,2},{4,5},{5,4},{6,7},{7,6},{8,9},{9,8},{10,11... | collective-permute-start | bytes 3145736 | tf_op jit(solution)/shard_map/ppermute | solution.py:765
  319.3 26.5 %collective-permute-start.20 = (bf16[512,1024]{1,0:T(8,128)(2,1)}, bf16[512,1024]{1,0:T(8,128)(2,1)}, u32[]{:S(2)}, u32[]{:S(2)}) collective-permute-start(bf16[512,1024]{1,0:T(8,128)(2,1)} %get-tuple-element.42), channel_id=1, source_target_pairs={{0,4},{2,6},{4,0},{6,2},{1,5},{3,7},{5,1},{7,3},{8,12},{10,14},{12... | collective-permute-start | bytes 3145736 | tf_op jit(solution)/shard_map/ppermute | solution.py:765
  321.0 64.9 %collective-permute-start.21 = (bf16[512,1024]{1,0:T(8,128)(2,1)}, bf16[512,1024]{1,0:T(8,128)(2,1)}, u32[]{:S(2)}, u32[]{:S(2)}) collective-permute-start(bf16[512,1024]{1,0:T(8,128)(2,1)} %get-tuple-element.44), channel_id=1, source_target_pairs={{0,4},{2,6},{4,0},{6,2},{1,5},{3,7},{5,1},{7,3},{8,12},{10,14},{12... | collective-permute-start | bytes 3145736 | tf_op jit(solution)/shard_map/ppermute | solution.py:765
  328.7 38.8 %all-to-all-start.2 = ((f32[16,2,128]{2,1,0:T(2,128)}), f32[16,2,128]{2,1,0:T(2,128)S(1)}, u32[]{:S(2)}, u32[]{:S(2)}) async-start(f32[16,2,128]{2,1,0:T(2,128)} %maximum_bitcast_fusion), calls=%async_computation.2 | async-start | bytes 32768 | tf_op jit(solution)/shard_map/all_to_all | solution.py:868
  367.5 35.0 %all-to-all-start.5 = ((bf16[4,128,1024]{2,1,0:T(8,128)(2,1)}), bf16[4,128,1024]{2,1,0:T(8,128)(2,1)S(1)}, u32[]{:S(2)}, u32[]{:S(2)}) async-start(bf16[4,128,1024]{2,1,0:T(8,128)(2,1)} %bitcast.79), calls=%async_computation.5 | async-start | bytes 2097152 | tf_op jit(solution)/shard_map/all_to_all | solution.py:839
  380.6 58.5 %collective-permute-start.4 = (bf16[4,2,128,1536]{3,2,1,0:T(8,128)(2,1)}, bf16[4,2,128,1536]{3,2,1,0:T(8,128)(2,1)}, u32[]{:S(2)}, u32[]{:S(2)}) collective-permute-start(bf16[4,2,128,1536]{3,2,1,0:T(8,128)(2,1)} %dynamic-slice_bitcast_fusion), channel_id=1, source_target_pairs={{0,2},{2,0},{4,6},{6,4},{1,3},{3,1},{5,7},{7,5},{8,10},{10,8},{12,... | collective-permute-start | bytes 9437192 | tf_op jit(solution)/shard_map/ppermute | solution.py:765
  385.2 28.9 %collective-permute-start.6 = (bf16[4,2,128,1024]{3,2,0,1:T(8,128)(2,1)}, bf16[4,2,128,1024]{3,2,0,1:T(8,128)(2,1)}, u32[]{:S(2)}, u32[]{:S(2)}) collective-permute-start(bf16[4,2,128,1024]{3,2,0,1:T(8,128)(2,1)} %bitcast.71), channel_id=1, source_target_pairs={{0,2},{2,0},{4,6},{6,4},{1,3},{3,1},{5,7},{7,5},{8,10},{10,8},{12,... | collective-permute-start | bytes 6291464 | tf_op jit(solution)/shard_map/ppermute | solution.py:765
  385.7 25.4 %collective-permute-start.22 = (bf16[512,1024]{1,0:T(8,128)(2,1)}, bf16[512,1024]{1,0:T(8,128)(2,1)}, u32[]{:S(2)}, u32[]{:S(2)}) collective-permute-start(bf16[512,1024]{1,0:T(8,128)(2,1)} %get-tuple-element.46), channel_id=1, source_target_pairs={{0,4},{2,6},{4,0},{6,2},{1,5},{3,7},{5,1},{7,3},{8,12},{10,14},{12... | collective-permute-start | bytes 3145736 | tf_op jit(solution)/shard_map/ppermute | solution.py:765
  402.6 29.6 %all-to-all-start.6 = ((bf16[4,128,1024]{2,1,0:T(8,128)(2,1)}), bf16[4,128,1024]{2,1,0:T(8,128)(2,1)}, u32[]{:S(2)}, u32[]{:S(2)}) async-start(bf16[4,128,1024]{2,1,0:T(8,128)(2,1)} %bitcast.77), calls=%async_computation.6 | async-start | bytes 2097152 | tf_op jit(solution)/shard_map/all_to_all | solution.py:839
  432.2 35.8 %all-to-all-start.7 = ((bf16[4,128,1024]{2,1,0:T(8,128)(2,1)}), bf16[4,128,1024]{2,1,0:T(8,128)(2,1)}, u32[]{:S(2)}, u32[]{:S(2)}) async-start(bf16[4,128,1024]{2,1,0:T(8,128)(2,1)} %bitcast.78), calls=%async_computation.7 | async-start | bytes 2097152 | tf_op jit(solution)/shard_map/all_to_all | solution.py:839
  438.7 26.3 %collective-permute-start.7 = (bf16[4,1,128,1024]{3,2,0,1:T(8,128)(2,1)}, bf16[4,1,128,1024]{3,2,0,1:T(8,128)(2,1)}, u32[]{:S(2)}, u32[]{:S(2)}) collective-permute-start(bf16[4,1,128,1024]{3,2,0,1:T(8,128)(2,1)} %constant_dynamic-slice_fusion.1), channel_id=1, source_target_pairs={{0,4},{2,6},{4,0},{6,2},{1,5},{3,7},{5,1},{7,3},{8,12},{10,14},{12... | collective-permute-start | bytes 3145736 | tf_op jit(solution)/shard_map/ppermute | solution.py:765
  445.6 51.3 %collective-permute-start.5 = (bf16[4,1,128,1536]{3,2,1,0:T(8,128)(2,1)}, bf16[4,1,128,1536]{3,2,1,0:T(8,128)(2,1)}, u32[]{:S(2)}, u32[]{:S(2)}) collective-permute-start(bf16[4,1,128,1536]{3,2,1,0:T(8,128)(2,1)} %constant_dynamic-slice_fusion.4), channel_id=1, source_target_pairs={{0,4},{2,6},{4,0},{6,2},{1,5},{3,7},{5,1},{7,3},{8,12},{10,14},{12... | collective-permute-start | bytes 4718600 | tf_op jit(solution)/shard_map/ppermute | solution.py:765
  468.0 32.4 %all-to-all-start.4 = ((bf16[4,128,1024]{2,1,0:T(8,128)(2,1)}), bf16[4,128,1024]{2,1,0:T(8,128)(2,1)}, u32[]{:S(2)}, u32[]{:S(2)}) async-start(bf16[4,128,1024]{2,1,0:T(8,128)(2,1)} %fusion.17), calls=%async_computation.4 | async-start | bytes 2097152 | tf_op jit(solution)/shard_map/all_to_all | solution.py:793
  500.4 40.3 %all-to-all-start.3 = ((bf16[4,128,1536]{2,1,0:T(8,128)(2,1)}), bf16[4,128,1536]{2,1,0:T(8,128)(2,1)}, u32[]{:S(2)}, u32[]{:S(2)}) async-start(bf16[4,128,1536]{2,1,0:T(8,128)(2,1)} %fusion.15), calls=%async_computation.3 | async-start | bytes 3145728 | tf_op jit(solution)/shard_map/all_to_all | solution.py:793
  (34 other events, 832.0 us)
Sparse Core Ops, SparseCore 0:
  19.7 19.4 all-gather.1
